TPU v7x, 1024 devices: a whole 8x8x8 slice. The times are simulated.
1024 devices in a mesh: dp: 64 (over z, y), pipe: 2 (over core), tensor: 8 (over x).
Axes of the slice: x: 8, y: 8, z: 8, core: 2. Of those that a mesh axis runs over, the one named last changes fastest.
Arguments:
- saved_inputs: bfloat16 [2, 64, 128, 1536], P('pipe', 'dp'), may hold values from -40 to 40
- cotangent: bfloat16 [64, 128, 1536], P('dp'), may hold values from -6 to 6
- frame_counts: int32 [64], P('dp'), may hold values from 1 to 128, 5120 in all
- glu_weight: bfloat16 [2, 1536, 2, 1536], P('pipe', None, None, 'tensor'), may hold values from -0.15625 to 0.15625
- conv_kernel: float32 [2, 32, 1536], P('pipe', None, 'tensor'), may hold values from -1 to 1
- norm_gain: float32 [2, 1536], P('pipe', 'tensor'), may hold values from 0.5 to 1.5
- norm_bias: float32 [2, 1536], P('pipe', 'tensor'), may hold values from -3 to 3
- out_weight: bfloat16 [2, 1536, 1536], P('pipe', None, 'tensor'), may hold values from -0.15625 to 0.15625
Outputs:
- input_grads: bfloat16 [2, 64, 128, 1536], P('pipe', 'dp', None, 'tensor')
- glu_weight_grad: float32 [2, 1536, 2, 1536], P('pipe', 'dp', None, 'tensor')
- out_weight_grad: float32 [2, 1536, 1536], P('pipe', 'dp', 'tensor')
- kernel_grad: float32 [2, 32, 1536], P('pipe', None, 'tensor')
- gain_grad: float32 [2, 1536], P('pipe', 'tensor')
- bias_grad: float32 [2, 1536], P('pipe', 'tensor')
Inputs may be any that keep to these rules, and one draw needn't show every extreme that they name: frame_counts: each utterance has 1 to 128 valid frames and some utterance has exactly 128; slots at or past an utterance's count are padding.
All inputs are finite; a program needn't handle non-finite values. No bound on the sum of `frame_counts` on one device may be relied on, other than what follows from the above.
Results may differ from a plain program's by a relative error of at most 0.01.
Values may be sent and summed in bfloat16 or wider, within the bound.
A program may use at most 64 MiB of HBM per device.

v0:
```python
import jax
import jax.numpy as jnp
from jax import lax
from jax.sharding import PartitionSpec as P

D = 1536
KERNEL = 32


EPSILON = 1e-05


def shifted(shard, axis, by):
    devices = lax.axis_size(axis)
    pairs = [(i, i + by) for i in range(devices) if 0 <= i + by < devices]
    return lax.ppermute(shard, axis, pairs)


def depthwise(signal, taps, low_pad, high_pad, channels):
    return lax.conv_general_dilated(
        signal,
        taps[:, None, :],
        window_strides=(1,),
        padding=[(low_pad, high_pad)],
        dimension_numbers=("NWC", "WIO", "NWC"),
        feature_group_count=channels,
        precision=lax.Precision.HIGHEST,
    )


def shards(
    saved_inputs, cotangent, frame_counts, glu_weight, conv_kernel, norm_gain, norm_bias, out_weight
):
    channels = D // lax.axis_size("tensor")
    tensor_index = lax.axis_index("tensor")
    pipe_index = lax.axis_index("pipe")
    inputs = saved_inputs[0]
    utterances = inputs.shape[0]
    frames = inputs.shape[1]
    left_pad = KERNEL // 2
    positions = jnp.arange(frames, dtype=jnp.int32)
    validity = (positions[None, :] < frame_counts[:, None]).astype(jnp.float32)[..., None]
    glu_flat = glu_weight[0].reshape(D, 2 * channels)
    kernel_taps = conv_kernel[0]
    gain_local = norm_gain[0]
    bias_local = norm_bias[0]
    back_weight = out_weight[0]
    inputs_flat = inputs.reshape(-1, D)
    projected = jnp.dot(inputs_flat, glu_flat, preferred_element_type=jnp.float32).reshape(
        utterances, frames, 2, channels
    )
    gated = projected[:, :, 0] * jax.nn.sigmoid(projected[:, :, 1]) * validity
    convolved = depthwise(gated, kernel_taps, left_pad, KERNEL - 1 - left_pad, channels)
    moment_sums = lax.psum(
        (
            jnp.sum(convolved * validity, axis=(0, 1)),
            jnp.sum(convolved * convolved * validity, axis=(0, 1)),
            jnp.sum(validity),
        ),
        "dp",
    )
    frame_total = moment_sums[2]
    center = moment_sums[0] / frame_total
    inv_std = lax.rsqrt(moment_sums[1] / frame_total - center * center + EPSILON)
    normed = (convolved - center) * inv_std
    scaled = gain_local * normed + bias_local
    squash = jax.nn.sigmoid(scaled)
    activated = (scaled * squash * validity).astype(jnp.bfloat16)
    padded = jnp.pad(gated, ((0, 0), (left_pad, KERNEL - 1 - left_pad), (0, 0)))
    windows = jnp.stack([padded[:, tap_index : tap_index + frames] for tap_index in range(KERNEL)])
    validity_full = jnp.broadcast_to(validity, normed.shape)
    squash_b = jax.nn.sigmoid(projected[:, :, 1])

    def backward(upstream, with_weights):
        grad_act = jnp.dot(
            upstream.reshape(-1, D), back_weight, preferred_element_type=jnp.float32
        ).reshape(utterances, frames, channels)
        grad_scaled = grad_act * validity * squash * (1.0 + scaled * (1.0 - squash))
        stacked = jnp.stack([grad_scaled, validity_full, validity_full * normed])
        tap_sums = jnp.einsum("jutc,kutc->jkc", stacked, windows, precision=lax.Precision.HIGHEST)
        bias_grad, gain_grad, tap_sums = lax.psum(
            (
                jnp.sum(grad_scaled, axis=(0, 1)),
                jnp.sum(grad_scaled * normed, axis=(0, 1)),
                tap_sums,
            ),
            "dp",
        )
        factor = gain_local * inv_std
        grad_conv = (
            factor
            * (grad_scaled - bias_grad / frame_total - normed * gain_grad / frame_total)
            * validity
        )
        kernel_grad = factor * (
            tap_sums[0]
            - bias_grad / frame_total * tap_sums[1]
            - gain_grad / frame_total * tap_sums[2]
        )
        grad_gated = (
            depthwise(grad_conv, kernel_taps[::-1], KERNEL - 1 - left_pad, left_pad, channels)
            * validity
        )
        grad_proj = jnp.stack(
            [grad_gated * squash_b, grad_gated * projected[:, :, 0] * squash_b * (1.0 - squash_b)],
            axis=2,
        ).astype(jnp.bfloat16)
        grad_flat = grad_proj.reshape(-1, 2 * channels)
        reduced = lax.psum_scatter(
            lax.dot_general(
                glu_flat, grad_flat, (((1,), (1,)), ((), ())), preferred_element_type=jnp.float32
            ).astype(jnp.bfloat16),
            "tensor",
            scatter_dimension=0,
            tiled=True,
        ).astype(jnp.float32)
        upstream_part = lax.dynamic_slice_in_dim(upstream, tensor_index * channels, channels, 2)
        input_grad = (
            upstream_part.astype(jnp.float32) + reduced.T.reshape(utterances, frames, channels)
        ).astype(jnp.bfloat16)
        if not with_weights:
            return (input_grad, None)
        glu_grad = lax.dot_general(
            inputs_flat, grad_flat, (((0,), (0,)), ((), ())), preferred_element_type=jnp.float32
        ).reshape(1, D, 2, channels)
        out_grad = lax.dot_general(
            upstream.reshape(-1, D),
            activated.reshape(-1, channels),
            (((0,), (0,)), ((), ())),
            preferred_element_type=jnp.float32,
        ).reshape(1, D, channels)
        return (input_grad, (glu_grad, out_grad, kernel_grad, gain_grad, bias_grad))

    first_grad = backward(cotangent, False)[0]
    whole = lax.all_gather(first_grad, "tensor", axis=2, tiled=True)
    arrived = shifted(whole, "pipe", -1)
    upstream_now = jnp.where(pipe_index == 1, cotangent, arrived)
    final_grad, weight_parts = backward(upstream_now, True)
    input_grads = final_grad[None]
    glu_grad, out_grad, kernel_grad, gain_grad, bias_grad = weight_parts
    glu_shard, out_shard = (
        lax.psum_scatter(glu_grad, "dp", scatter_dimension=1, tiled=True),
        lax.psum_scatter(out_grad, "dp", scatter_dimension=1, tiled=True),
    )
    return (input_grads, glu_shard, out_shard, kernel_grad[None], gain_grad[None], bias_grad[None])


def solution(mesh):
    placed = (
        P("pipe", "dp", None, None),
        P("dp", None, None),
        P("dp"),
        P("pipe", None, None, "tensor"),
        P("pipe", None, "tensor"),
        P("pipe", "tensor"),
        P("pipe", "tensor"),
        P("pipe", None, "tensor"),
    )
    return jax.shard_map(
        shards,
        mesh=mesh,
        in_specs=placed,
        out_specs=(
            P("pipe", "dp", None, "tensor"),
            P("pipe", "dp", None, "tensor"),
            P("pipe", "dp", "tensor"),
            P("pipe", None, "tensor"),
            P("pipe", "tensor"),
            P("pipe", "tensor"),
        ),
        check_vma=False,
    )
```

profile of v0, /device:TPU:14, one launch (start us, length us, event | category | flops | bytes accessed | tf_op | source)
XLA Modules:
  0.0 766.3 jit_solution(5375775851854082646)
XLA Ops:
  8.5 1.5 fusion.13
  10.1 1.3 fusion.122
  12.3 157.7 %all-reduce.5 = (f32[192]{0:T(256)S(1)}, f32[]{:T(128)}, f32[192]{0:T(256)S(1)}) all-reduce(f32[192]{0:T(256)S(1)} %get-tuple-element.25, f32[]{:T(128)} %fusion.128, f32[192]{0:T(256)S(1)} %get-tuple-element.24), channel_id=1, replica_groups=mesh['dp'=64,'pipe'=2,'tensor'=8] {'dp'}, use_global_device_ids=true, to_apply=%region_5.0 | all-reduce | flops 385 | bytes 3080 | tf_op jit(solution)/shard_map/psum | solution.py:54
  171.1 138.0 %all-reduce.4 = (f32[192]{0:T(256)S(1)}, f32[192]{0:T(256)S(1)}) all-reduce(f32[192]{0:T(256)S(1)} %get-tuple-element.29, f32[192]{0:T(256)S(1)} %get-tuple-element.28), channel_id=1, replica_groups=mesh['dp'=64,'pipe'=2,'tensor'=8] {'dp'}, use_global_device_ids=true, to_apply=%region_9.10 | all-reduce | flops 384 | bytes 3072 | tf_op jit(solution)/shard_map/psum | solution.py:81
  309.8 1.5 multiply_bitcast_fusion
  312.5 0.9 copy.74
  333.8 14.4 %reduce-scatter.8.cloned.1.call-done = bf16[192,128]{1,0:T(8,128)(2,1)} async-done(((bf16[1536,128]{1,0:T(8,128)(2,1)}), bf16[192,128]{1,0:T(8,128)(2,1)}) %reduce-scatter.8.cloned.1.call-update) | async-done | bytes 49168
  348.2 0.9 copy.75
  349.3 25.0 %all_gather.3 = bf16[1,128,1536]{1,2,0:T(8,128)(2,1)S(1)} all-gather(bf16[1,128,192]{1,2,0:T(8,128)(2,1)S(1)} %copy.62), channel_id=1, replica_groups=mesh['dp'=64,'pipe'=2,'tensor'=8] {'tensor'}, dimensions={2}, use_global_device_ids=true | all-gather | bytes 442368 | tf_op jit(solution)/shard_map/all_gather | solution.py:135
  374.4 1.3 collective-permute-start
  379.6 1.6 fusion.132
  381.2 144.0 %all-reduce.3 = (f32[192]{0:T(256)S(1)}, f32[192]{0:T(256)S(1)}) all-reduce(f32[192]{0:T(256)S(1)} %get-tuple-element.27, f32[192]{0:T(256)S(1)} %get-tuple-element.26), channel_id=1, replica_groups=mesh['dp'=64,'pipe'=2,'tensor'=8] {'dp'}, use_global_device_ids=true, to_apply=%region_14.15 | all-reduce | flops 384 | bytes 3072 | tf_op jit(solution)/shard_map/psum | solution.py:81
  527.9 0.9 copy.76
  529.0 1.4 fusion.28
  530.5 3.4 copy.68
  533.8 1.5 convolution_bitcast_fusion
  535.3 2.7 copy.69
  538.1 10.4 %fusion.6 = f32[3,32,192]{1,0,2:T(4,128)} fusion(f32[32,128,192]{1,2,0:T(8,128)} %bitcast.72, f32[3,128,192]{1,2,0:T(8,128)S(1)} %maximum_bitcast_fusion), kind=kOutput, calls=%fused_computation.40 | convolution fusion | flops 28311552 | bytes 3514368 | tf_op jit(solution)/shard_map/jutc,kutc->jkc/dot_general | solution.py:80
  548.6 1.3 dynamic-slice
  551.2 11.5 %reduce-scatter.10.cloned.1.call-done = bf16[192,128]{1,0:T(8,128)(2,1)} async-done(((bf16[1536,128]{1,0:T(8,128)(2,1)}), bf16[192,128]{1,0:T(8,128)(2,1)}) %reduce-scatter.10.cloned.1.call-update) | async-done | bytes 49168 | tf_op jit(solution)/shard_map/reduce_scatter | solution.py:109
  562.7 1.5 fusion.117
  564.2 189.9 %all-reduce.9.cloned.1.call-done = (f32[1,1536,2,192]{3,2,1,0:T(2,128)}, f32[1,1536,192]{2,0,1:T(1,128)}, f32[3,32,192]{1,0,2:T(4,128)}) async-done(((f32[1,1536,2,192]{3,2,1,0:T(2,128)}, f32[1,1536,192]{2,0,1:T(1,128)}, f32[3,32,192]{1,0,2:T(4,128)}), (f32[1,1536,2,192]{3,2,1,0:T(2,128)}, f32[1,1536,192]{2,0,1:T(1,128)}, f32[3,32,192]{1,0,2:T(4,128)})) %all-reduce.9.cloned.1.call-update) | async-done | bytes 3612688
  754.1 2.2 fusion.114
  757.0 1.4 constant_dynamic-slice_fusion.1
  (102 shorter events, 34.4 us)
Async XLA Ops:
  7.2 1.3 copy-start
  7.2 162.8 %copy-start.11 = (f32[1,192]{1,0:T(1,128)S(1)}, f32[1,192]{1,0:T(1,128)}, u32[]{:S(2)}) copy-start(f32[1,192]{1,0:T(1,128)} %param.13) | copy-start | bytes 2308
  7.2 163.4 %copy-start.12 = (f32[1,192]{1,0:T(1,128)S(1)}, f32[1,192]{1,0:T(1,128)}, u32[]{:S(2)}) copy-start(f32[1,192]{1,0:T(1,128)} %param.14) | copy-start | bytes 2308
  7.2 163.4 %copy-start.14 = (bf16[1,1536,192]{1,2,0:T(8,128)(2,1)S(1)}, bf16[1,1536,192]{1,2,0:T(8,128)(2,1)}, u32[]{:S(2)}) copy-start(bf16[1,1536,192]{1,2,0:T(8,128)(2,1)} %param.15) | copy-start | bytes 1769476
  7.2 163.4 %copy-start.2 = (bf16[1,128,1536]{2,1,0:T(8,128)(2,1)S(1)}, bf16[1,128,1536]{2,1,0:T(8,128)(2,1)}, u32[]{:S(2)}) copy-start(bf16[1,128,1536]{2,1,0:T(8,128)(2,1)} %param.9) | copy-start | bytes 1179652
  7.2 341.0 %reduce-scatter.8.cloned.1.call-start = ((), (), s32[]{:S(2)}) async-start(), calls=%async_computation.2 | async-start | bytes 442368
  8.5 302.9 %copy-start.6 = (f32[1,32,192]{2,1,0:T(8,128)S(1)}, f32[1,32,192]{2,1,0:T(8,128)}, u32[]{:S(2)}) copy-start(f32[1,32,192]{2,1,0:T(8,128)} %param.12) | copy-start | bytes 73732
  11.5 514.4 %copy-start.1 = (f32[1,128,192]{1,2,0:T(8,128)}, f32[1,128,192]{1,2,0:T(8,128)S(1)}, u32[]{:S(2)}) copy-start(f32[1,128,192]{1,2,0:T(8,128)S(1)} %copy.55) | copy-start | bytes 294916
  313.4 249.3 %reduce-scatter.10.cloned.1.call-start = ((), (), s32[]{:S(2)}) async-start(), calls=%async_computation.3 | async-start | bytes 442368 | tf_op jit(solution)/shard_map/reduce_scatter | solution.py:109
  374.4 4.4 collective-permute-start
  381.2 146.3 %copy-start.4 = (f32[1,128,192]{1,2,0:T(8,128)}, f32[1,128,192]{1,2,0:T(8,128)S(1)}, u32[]{:S(2)}) copy-start(f32[1,128,192]{1,2,0:T(8,128)S(1)} %get-tuple-element.50) | copy-start | bytes 294916
  525.2 3.8 copy-start.9
  525.2 3.8 copy-start.13
  525.9 3.1 copy-start.7
  528.9 225.2 %all-reduce.9.cloned.1.call-start = ((), (), s32[]{:S(2)}) async-start(), calls=%async_computation.4 | async-start | bytes 10223616
  533.8 4.3 copy-start.3
  533.8 4.3 copy-start.5
  548.6 2.0 copy-start.10
  548.6 205.5 %copy-start.8 = (f32[192]{0:T(256)S(1)}, f32[192]{0:T(256)}, u32[]{:S(2)}) copy-start(f32[192]{0:T(256)} %copy-done.7) | copy-start | bytes 2308
Sparse Core Ops, SparseCore 0:
  313.6 34.6 reduce-scatter.7
  529.0 33.6 reduce-scatter.9
  566.4 187.6 all-reduce.8
where the time goes:
time: 767 us; the launch traced here: 766 us
  blocking collectives  465 us (61%)
  waiting for transfers between devices  216 us (28%)
  local copies, waits for them, and re-layouts  37.6 us (5%)
  matrix products  20 us (3%)
  between operations  15.6 us (2%)
  other arithmetic  11 us (1%)
    psum x2, blocking collectives, backward(): lax.psum((jnp.sum(grad_scaled, axis=(0, 1)), jnp.sum(grad_scaled * normed...  282 us
    unnamed x5, waiting for transfers between devices  204 us
    psum x1, blocking collectives, shards(): lax.psum((jnp.sum(convolved * validity, axis=(0, 1)), jnp.sum(convolved *...  158 us
    unnamed x69, local copies, waits for them, and re-layouts  30 us
    all_gather x1, blocking collectives, shards(): whole = lax.all_gather(first_grad, 'tensor', axis=2, tiled=True)  25 us
  transfers between devices with their start and end apart: 4, of which 3 were waited for; matrix products, arithmetic and copies ran while one was open for 6% of the time, Pallas kernels for 0%

commit v1 on v0

v1 whole, which is shorter than its diff:
```python
import functools

import jax
import jax.numpy as jnp
from jax import lax
from jax.experimental import pallas as pl
from jax.experimental.pallas import tpu as pltpu
from jax.sharding import PartitionSpec as P

KERNEL = 32
EPSILON = 1e-05
FRAMES = 128
LANES = 128
NY = 8
PAD = 16

STAT_Y, STAT_Z, SUM_Y, SUM_Z, PART, GATHER = 0, 1, 2, 3, 4, 5
OUT_1, OUT_2, GLU_Y1, GLU_Z2, GLU_Z1, GLU_Y2, TAP_Z, TAP_Y = 6, 7, 8, 9, 10, 11, 12, 13
STAGES = 14


def body(
    nx, ny, nz, cnt_ref, x_ref, xt_ref, glu_ref, par_ref, owt_ref, cot_ref,
    ig_ref, gg_ref, og_ref, kg_ref, gb_ref,
    up, h0s, sgs, gpad, gcpad, convs, normeds, dacts, acts, gas, gss, gps,
    st_y, st_z, su_y, su_z, rx, share,
    gsend, gy1, gy1s, gz2, gz1, gz1s, gy2, osend, oy1, oy1s, oz2, tz, ty,
    local_sem, send_sem, recv_sem,
):
    dp = lax.axis_index("dp")
    core = lax.axis_index("pipe")
    mx = lax.axis_index("tensor")
    my = lax.rem(dp, ny)
    mz = lax.div(dp, ny)
    depth = x_ref.shape[1]
    channels = depth // nx
    rows = depth // (ny * nz)

    def at_x(i):
        return (dp, core, i)

    def at_y(i):
        return (mz * ny + i, core, mx)

    def at_z(i):
        return (i * ny + my, core, mx)

    axes = {"x": (mx, nx, at_x), "y": (my, ny, at_y), "z": (mz, nz, at_z)}

    def copy(stage, axis, r, src, dst):
        me, n, where = axes[axis]
        peer = lax.rem(me + r, n)
        return pltpu.make_async_remote_copy(
            src_ref=src(peer), dst_ref=dst(me),
            send_sem=send_sem.at[stage, r], recv_sem=recv_sem.at[stage, me],
            device_id=where(peer), device_id_type=pl.DeviceIdType.MESH,
        )

    def arrival(stage, axis, s, dst):
        me, n, where = axes[axis]
        return pltpu.make_async_remote_copy(
            src_ref=dst(s), dst_ref=dst(s),
            send_sem=send_sem.at[stage, 0], recv_sem=recv_sem.at[stage, s],
            device_id=where(lax.rem(me + 1, n)), device_id_type=pl.DeviceIdType.MESH,
        )

    def push(stage, axis, src, dst):
        n = axes[axis][1]

        @pl.loop(1, n)
        def _(r):
            copy(stage, axis, r, src, dst).start()

    def take(stage, axis, dst):
        me, n, _ = axes[axis]

        @pl.loop(1, n)
        def _(r):
            arrival(stage, axis, lax.rem(me + r, n), dst).wait_recv()

    def drain(stage, axis, src, dst):
        n = axes[axis][1]

        @pl.loop(1, n)
        def _(r):
            copy(stage, axis, r, src, dst).wait_send()

    barrier = pltpu.get_barrier_semaphore()
    for axis in ("x", "y", "z"):
        me, n, where = axes[axis]

        @pl.loop(1, n)
        def _(r):
            pl.semaphore_signal(
                barrier, inc=1, device_id=where(lax.rem(me + r, n)),
                device_id_type=pl.DeviceIdType.MESH,
            )

    @pl.loop(0, nx)
    def _(i):
        pl.semaphore_signal(
            barrier, inc=1, device_id=(dp, 1 - core, i), device_id_type=pl.DeviceIdType.MESH
        )

    @pl.when(core == 1)
    def _():
        pltpu.make_async_copy(cot_ref, up, local_sem).start()

    count = cnt_ref[0]
    frame = lax.broadcasted_iota(jnp.int32, (FRAMES, LANES), 0)
    lane = lax.broadcasted_iota(jnp.int32, (FRAMES, LANES), 1)
    valid = (frame < count).astype(jnp.float32)
    low = lane < LANES // 2
    zero_pad = jnp.zeros((PAD, LANES), jnp.float32)

    projected = jnp.dot(x_ref[...], glu_ref[...].reshape(depth, 3 * LANES), preferred_element_type=jnp.float32)
    p0, p1, p2 = (projected[:, i * LANES : (i + 1) * LANES] for i in range(3))
    values = (p0, jnp.where(low, p2, 0.0))
    gates = (p1, jnp.where(low, pltpu.roll(p2, LANES // 2, 1), 0.0))
    for j in range(2):
        squash_b = jax.nn.sigmoid(gates[j])
        h0s[j] = values[j]
        sgs[j] = squash_b
        gpad[j, 0:PAD, :] = zero_pad
        gpad[j, PAD + FRAMES :, :] = zero_pad
        gpad[j, PAD : PAD + FRAMES, :] = values[j] * squash_b * valid
    for j in range(2):
        acc = jnp.zeros((FRAMES, LANES), jnp.float32)
        for b in range(8):
            window = gpad[j, pl.ds(b, FRAMES + 24), :]
            for a in range(KERNEL // 8):
                acc = acc + par_ref[j, pl.ds(8 * a + b, 1), :] * window[8 * a : 8 * a + FRAMES]
        convs[j] = acc
        masked = acc * valid
        st_y[my, pl.ds(j, 1), :] = jnp.sum(masked, axis=0, keepdims=True)
        st_y[my, pl.ds(2 + j, 1), :] = jnp.sum(masked * acc, axis=0, keepdims=True)
    st_y[my, pl.ds(4, 4), :] = jnp.full((4, LANES), count, jnp.int32).astype(jnp.float32)

    pl.semaphore_wait(barrier, (nx - 1) + (ny - 1) + (nz - 1) + nx)

    def small_start(stage, buf):
        push(stage, "y", lambda i: buf.at[my], lambda i: buf.at[i])

    def summed(buf, n):
        total = buf[0]
        for s in range(1, n):
            total = total + buf[s]
        return total

    def small_finish(stage, buf, buf2):
        take(stage, "y", lambda i: buf.at[i])
        buf2[mz] = summed(buf, ny)
        push(stage + 1, "z", lambda i: buf2.at[mz], lambda i: buf2.at[i])
        take(stage + 1, "z", lambda i: buf2.at[i])
        return summed(buf2, nz)

    def small_drain(stage, buf, buf2):
        drain(stage, "y", lambda i: buf.at[my], lambda i: buf.at[i])
        drain(stage + 1, "z", lambda i: buf2.at[mz], lambda i: buf2.at[i])

    def grad_act():
        flat = up[...].reshape(depth, FRAMES)
        ga = jnp.dot(owt_ref[...], flat, preferred_element_type=jnp.float32)
        for j in range(2):
            gas[j] = jnp.transpose(ga[j * LANES : (j + 1) * LANES])

    small_start(STAT_Y, st_y)

    @pl.when(core == 1)
    def _():
        pltpu.make_async_copy(cot_ref, up, local_sem).wait()
        grad_act()

    stats = small_finish(STAT_Y, st_y, st_z)
    total = stats[4:5]
    factors = []
    for j in range(2):
        gain = par_ref[j, pl.ds(KERNEL, 1), :]
        shift = par_ref[j, pl.ds(KERNEL + 1, 1), :]
        center = stats[j : j + 1] / total
        inv_std = lax.rsqrt(stats[2 + j : 3 + j] / total - center * center + EPSILON)
        factors.append(gain * inv_std)
        normed = (convs[j] - center) * inv_std
        scaled = gain * normed + shift
        squash = jax.nn.sigmoid(scaled)
        normeds[j] = normed
        dacts[j] = valid * squash * (1.0 + scaled * (1.0 - squash))
        acts[:, j * LANES : (j + 1) * LANES] = (scaled * squash * valid).astype(jnp.bfloat16)

    def gather_copy(i):
        return pltpu.make_async_remote_copy(
            src_ref=share, dst_ref=up.at[mx],
            send_sem=send_sem.at[GATHER, i], recv_sem=recv_sem.at[GATHER, mx],
            device_id=(dp, 0, i), device_id_type=pl.DeviceIdType.MESH,
        )

    @pl.when(core == 0)
    def _():
        @pl.loop(0, nx)
        def _(i):
            pltpu.make_async_remote_copy(
                src_ref=share, dst_ref=up.at[i],
                send_sem=send_sem.at[GATHER, 0], recv_sem=recv_sem.at[GATHER, i],
                device_id=(dp, 1, i), device_id_type=pl.DeviceIdType.MESH,
            ).wait_recv()

        grad_act()

    for j in range(2):
        gs = gas[j] * dacts[j]
        gss[j] = gs
        su_y[my, pl.ds(j, 1), :] = jnp.sum(gs, axis=0, keepdims=True)
        su_y[my, pl.ds(2 + j, 1), :] = jnp.sum(gs * normeds[j], axis=0, keepdims=True)
    su_y[my, pl.ds(4, 4), :] = jnp.zeros((4, LANES), jnp.float32)
    small_start(SUM_Y, su_y)

    @pl.loop(0, nz)
    def _(z):
        left = up[...] if nz == 1 else out_rows(up, z, nz)
        block = jnp.dot(left, acts[...], preferred_element_type=jnp.float32)
        for i in range(2):
            osend[i, z] = block[:, i * LANES : (i + 1) * LANES].reshape(ny, rows, LANES).astype(jnp.bfloat16)

    o_src = lambda i: osend.at[:, :, i]
    o_dst = lambda i: oy1.at[i]
    push(OUT_1, "y", o_src, o_dst)

    sums = small_finish(SUM_Y, su_y, su_z)
    gb_ref[...] = sums
    for j in range(2):
        gcpad[j, 0:PAD, :] = zero_pad
        gcpad[j, PAD + FRAMES :, :] = zero_pad
        gcpad[j, PAD : PAD + FRAMES, :] = (
            factors[j]
            * (gss[j] - sums[j : j + 1] / total - normeds[j] * (sums[2 + j : 3 + j] / total))
            * valid
        )
    halves = []
    for j in range(2):
        acc = jnp.zeros((FRAMES, LANES), jnp.float32)
        for b in range(8):
            first = 1 if b == 0 else 0
            window = gcpad[j, pl.ds(b, FRAMES + 24 + 8 * first), :]
            for a in range(first, first + KERNEL // 8):
                k = KERNEL - 8 * a - b
                acc = acc + par_ref[j, pl.ds(k, 1), :] * window[8 * a : 8 * a + FRAMES]
        gg = acc * valid * sgs[j]
        halves.append((gg, gg * h0s[j] * (1.0 - sgs[j])))
    gps[:, 0:LANES] = halves[0][0].astype(jnp.bfloat16)
    gps[:, LANES : 2 * LANES] = halves[0][1].astype(jnp.bfloat16)
    gps[:, 2 * LANES :] = (halves[1][0] + pltpu.roll(halves[1][1], LANES // 2, 1)).astype(jnp.bfloat16)

    def part_copy(i):
        return pltpu.make_async_remote_copy(
            src_ref=rx.at[1, i], dst_ref=rx.at[0, mx],
            send_sem=send_sem.at[PART, i], recv_sem=recv_sem.at[PART, mx],
            device_id=at_x(i), device_id_type=pl.DeviceIdType.MESH,
        )

    def partial_of(i):
        return lax.dot_general(
            glu_ref[i], gps[...], (((1,), (1,)), ((), ())), preferred_element_type=jnp.float32
        ).astype(jnp.bfloat16)

    @pl.loop(1, nx)
    def _(r):
        i = lax.rem(mx + r, nx)
        rx[1, i] = partial_of(i)
        part_copy(i).start()

    rx[0, mx] = partial_of(mx)

    @pl.loop(0, nz)
    def _(z):
        block = jnp.dot(xt_ref[z], gps[...], preferred_element_type=jnp.float32)
        for i in range(3):
            gsend[i, z] = block[:, i * LANES : (i + 1) * LANES].reshape(ny, rows, LANES).astype(jnp.bfloat16)

    gy_src = lambda i: gsend.at[0:2, :, i]
    gy_dst = lambda i: gy1.at[i]
    gz_src = lambda i: gsend.at[2, i]
    gz_dst = lambda i: gz1.at[i]
    push(GLU_Y1, "y", gy_src, gy_dst)
    push(GLU_Z1, "z", gz_src, gz_dst)

    for j in range(2):
        gc = gcpad[j, PAD : PAD + FRAMES, :]
        for b in range(8):
            window = gpad[j, pl.ds(b, FRAMES + 24), :]
            for a in range(KERNEL // 8):
                tz[mz, j, pl.ds(8 * a + b, 1), :] = jnp.sum(
                    gc * window[8 * a : 8 * a + FRAMES], axis=0, keepdims=True
                )
    tz_src = lambda i: tz.at[mz]
    tz_dst = lambda i: tz.at[i]
    push(TAP_Z, "z", tz_src, tz_dst)

    @pl.loop(1, nx)
    def _(r):
        i = lax.rem(mx + r, nx)
        arrival(PART, "x", i, lambda s: rx.at[0, s]).wait_recv()

    acc = rx[0, 0].astype(jnp.float32)
    for s in range(1, nx):
        acc = acc + rx[0, s].astype(jnp.float32)
    final = (up[mx].astype(jnp.float32) + acc).astype(jnp.bfloat16)
    share[...] = final
    ig_ref[...] = final

    @pl.when(core == 1)
    def _():
        @pl.loop(0, nx)
        def _(i):
            gather_copy(i).start()

    def reduce1(stage, axis, dst, own, sent):
        take(stage, axis, dst)
        me, n, _ = axes[axis]
        total = own.astype(jnp.float32)
        for r in range(1, n):
            total = total + dst(lax.rem(me + r, n))[...].astype(jnp.float32)
        sent[...] = total.astype(jnp.bfloat16)

    def reduce2(stage, axis, dst, own):
        take(stage, axis, dst)
        me, n, _ = axes[axis]
        total = own.astype(jnp.float32)
        for r in range(1, n):
            total = total + dst(lax.rem(me + r, n))[...].astype(jnp.float32)
        return total

    o2_src = lambda i: oy1s.at[:, i]
    o2_dst = lambda i: oz2.at[i]
    reduce1(OUT_1, "y", o_dst, osend[:, :, my], oy1s)
    push(OUT_2, "z", o2_src, o2_dst)

    take(TAP_Z, "z", tz_dst)
    ty[my] = summed(tz, nz)
    ty_src = lambda i: ty.at[my]
    ty_dst = lambda i: ty.at[i]
    push(TAP_Y, "y", ty_src, ty_dst)

    gy2_src = lambda i: gz1s.at[i]
    gy2_dst = lambda i: gy2.at[i]
    reduce1(GLU_Z1, "z", gz_dst, gsend[2, mz], gz1s)
    push(GLU_Y2, "y", gy2_src, gy2_dst)

    gz2_src = lambda i: gy1s.at[:, i]
    gz2_dst = lambda i: gz2.at[i]
    reduce1(GLU_Y1, "y", gy_dst, gsend[0:2, :, my], gy1s)
    push(GLU_Z2, "z", gz2_src, gz2_dst)

    og_ref[...] = reduce2(OUT_2, "z", o2_dst, oy1s[:, mz])
    take(TAP_Y, "y", ty_dst)
    kg_ref[...] = summed(ty, ny)
    gg_ref[2] = reduce2(GLU_Y2, "y", gy2_dst, gz1s[my])
    gg_ref[0:2] = reduce2(GLU_Z2, "z", gz2_dst, gy1s[:, mz])

    small_drain(STAT_Y, st_y, st_z)
    small_drain(SUM_Y, su_y, su_z)
    drain(OUT_1, "y", o_src, o_dst)

    @pl.loop(1, nx)
    def _(r):
        part_copy(lax.rem(mx + r, nx)).wait_send()

    drain(GLU_Y1, "y", gy_src, gy_dst)
    drain(GLU_Z1, "z", gz_src, gz_dst)
    drain(TAP_Z, "z", tz_src, tz_dst)

    @pl.when(core == 1)
    def _():
        @pl.loop(0, nx)
        def _(i):
            gather_copy(i).wait_send()

    drain(OUT_2, "z", o2_src, o2_dst)
    drain(TAP_Y, "y", ty_src, ty_dst)
    drain(GLU_Y2, "y", gy2_src, gy2_dst)
    drain(GLU_Z2, "z", gz2_src, gz2_dst)


def out_rows(up, z, nz):
    nx, channels, frames = up.shape
    if nx == nz:
        return up[z]
    rows = nx * channels // nz
    return up[...].reshape(nx * channels, frames)[:rows]


def shards(
    ny, saved_inputs, cotangent, frame_counts, glu_weight, conv_kernel, norm_gain, norm_bias, out_weight
):
    nx = lax.axis_size("tensor")
    nz = lax.axis_size("dp") // ny
    depth = saved_inputs.shape[-1]
    channels = depth // nx
    rows = depth // (ny * nz)
    half = LANES // 2
    inputs = saved_inputs[0, 0]
    glu = glu_weight[0]
    first, second = glu[:, 0], glu[:, 1]
    packed = jnp.concatenate(
        [first[:, :LANES], second[:, :LANES], first[:, LANES:], second[:, LANES:]], axis=1
    ).reshape(nx, channels, 3 * LANES)
    params = jnp.concatenate([conv_kernel[0], norm_gain, norm_bias], axis=0)
    params = jnp.pad(params, ((0, 6), (0, 2 * LANES - channels)))
    params = params.reshape(KERNEL + 8, 2, LANES).transpose(1, 0, 2)
    out_t = jnp.pad(out_weight[0].T, ((0, 2 * LANES - channels), (0, 0)))
    cot_t = cotangent[0].T.reshape(nx, channels, FRAMES)
    inputs_t = inputs.T.reshape(nz, depth // nz, FRAMES)

    f32, bf16 = jnp.float32, jnp.bfloat16
    vmem = pl.BlockSpec(memory_space=pltpu.VMEM)
    results = pl.pallas_call(
        functools.partial(body, nx, ny, nz),
        out_shape=(
            jax.ShapeDtypeStruct((channels, FRAMES), bf16),
            jax.ShapeDtypeStruct((3, rows, LANES), f32),
            jax.ShapeDtypeStruct((2, rows, LANES), f32),
            jax.ShapeDtypeStruct((2, KERNEL, LANES), f32),
            jax.ShapeDtypeStruct((8, LANES), f32),
        ),
        in_specs=[pl.BlockSpec(memory_space=pltpu.SMEM)] + [vmem] * 5 + [pl.BlockSpec(memory_space=pl.ANY)],
        out_specs=(vmem,) * 5,
        scratch_shapes=[
            pltpu.VMEM((nx, channels, FRAMES), bf16),
            pltpu.VMEM((2, FRAMES, LANES), f32),
            pltpu.VMEM((2, FRAMES, LANES), f32),
            pltpu.VMEM((2, FRAMES + 2 * PAD, LANES), f32),
            pltpu.VMEM((2, FRAMES + 2 * PAD, LANES), f32),
            pltpu.VMEM((2, FRAMES, LANES), f32),
            pltpu.VMEM((2, FRAMES, LANES), f32),
            pltpu.VMEM((2, FRAMES, LANES), f32),
            pltpu.VMEM((FRAMES, 2 * LANES), bf16),
            pltpu.VMEM((2, FRAMES, LANES), f32),
            pltpu.VMEM((2, FRAMES, LANES), f32),
            pltpu.VMEM((FRAMES, 3 * LANES), bf16),
            pltpu.VMEM((ny, 8, LANES), f32),
            pltpu.VMEM((nz, 8, LANES), f32),
            pltpu.VMEM((ny, 8, LANES), f32),
            pltpu.VMEM((nz, 8, LANES), f32),
            pltpu.VMEM((2, nx, channels, FRAMES), bf16),
            pltpu.VMEM((channels, FRAMES), bf16),
            pltpu.VMEM((3, nz, ny, rows, LANES), bf16),
            pltpu.VMEM((ny, 2, nz, rows, LANES), bf16),
            pltpu.VMEM((2, nz, rows, LANES), bf16),
            pltpu.VMEM((nz, 2, rows, LANES), bf16),
            pltpu.VMEM((nz, ny, rows, LANES), bf16),
            pltpu.VMEM((ny, rows, LANES), bf16),
            pltpu.VMEM((ny, rows, LANES), bf16),
            pltpu.VMEM((2, nz, ny, rows, LANES), bf16),
            pltpu.VMEM((ny, 2, nz, rows, LANES), bf16),
            pltpu.VMEM((2, nz, rows, LANES), bf16),
            pltpu.VMEM((nz, 2, rows, LANES), bf16),
            pltpu.VMEM((nz, 2, KERNEL, LANES), f32),
            pltpu.VMEM((ny, 2, KERNEL, LANES), f32),
            pltpu.SemaphoreType.DMA,
            pltpu.SemaphoreType.DMA((STAGES, max(nx, ny, nz))),
            pltpu.SemaphoreType.DMA((STAGES, max(nx, ny, nz))),
        ],
        compiler_params=pltpu.CompilerParams(collective_id=0, has_side_effects=True),
        name="conformer_backward",
    )(frame_counts, inputs, inputs_t, packed, params, out_t, cot_t)
    ig, gg, og, kg, gb = results
    input_grads = ig.T[None, None]
    tail = gg[2]
    glu_shard = jnp.stack(
        [
            jnp.concatenate([gg[0], tail[:, :half]], axis=1),
            jnp.concatenate([gg[1], tail[:, half:]], axis=1),
        ],
        axis=1,
    )[None]
    out_shard = jnp.concatenate([og[0], og[1][:, :half]], axis=1)[None]
    kernel_grad = jnp.concatenate([kg[0], kg[1][:, :half]], axis=1)[None]
    bias_grad = jnp.concatenate([gb[0], gb[1][:half]])[None]
    gain_grad = jnp.concatenate([gb[2], gb[3][:half]])[None]
    return (input_grads, glu_shard, out_shard, kernel_grad, gain_grad, bias_grad)


def solution(mesh):
    placed = (
        P("pipe", "dp", None, None),
        P("dp", None, None),
        P("dp"),
        P("pipe", None, None, "tensor"),
        P("pipe", None, "tensor"),
        P("pipe", "tensor"),
        P("pipe", "tensor"),
        P("pipe", None, "tensor"),
    )
    return jax.shard_map(
        functools.partial(shards, NY),
        mesh=mesh,
        in_specs=placed,
        out_specs=(
            P("pipe", "dp", None, "tensor"),
            P("pipe", "dp", None, "tensor"),
            P("pipe", "dp", "tensor"),
            P("pipe", None, "tensor"),
            P("pipe", "tensor"),
            P("pipe", "tensor"),
        ),
        check_vma=False,
    )
```

time: 767 us -> 105 us (0.14)
  blocking collectives: 465 us -> 0 us
  waiting for transfers between devices: 216 us -> 0 us
  Pallas kernels: 0 us -> 89.3 us
  local copies, waits for them, and re-layouts: 37.6 us -> 10.8 us
  matrix products: 20 us -> 0 us
  between operations: 15.6 us -> 1.39 us
  other arithmetic: 11 us -> 2.53 us
    psum x3 -> x0, blocking collectives: 440 us -> none  [the longest x2 282 us: backward(): lax.psum((jnp.sum(grad_scaled, axis=(0, 1)), jnp.sum(grad_scaled * normed...]
    unnamed x5 -> x0, waiting for transfers between devices: 204 us -> none
    pallas_call x0 -> x1, Pallas kernels: none -> 89.3 us  [shards(): pl.pallas_call(functools.partial(body, nx, ny, nz), out_shape=(jax.ShapeD...]
    unnamed x69 -> x14, local copies, waits for them, and re-layouts: 30 us -> 2.11 us
    all_gather x1 -> x0, blocking collectives: 25 us -> none  [shards(): whole = lax.all_gather(first_grad, 'tensor', axis=2, tiled=True)]
    dot_general x8 -> x0, matrix products: 17.7 us -> none  [the longest x1 10.4 us: backward(): jnp.einsum('jutc,kutc->jkc', stacked, windows, precision=lax.Precision.HI...]
    reduce_scatter x1 -> x0, waiting for transfers between devices: 11.5 us -> none  [backward(): lax.psum_scatter(lax.dot_general(glu_flat, grad_flat, (((1,), (1,)), ((),...]
  transfers between devices with their start and end apart: 4 -> 0, of which waited for: 3 -> 0; matrix products, arithmetic and copies ran while one was open for 6% -> 0% of each run, Pallas kernels for 0% -> 0%
where the time goes in v1:
time: 105 us; the launch traced here: 104 us
  Pallas kernels  89.3 us (85%)
  local copies, waits for them, and re-layouts  10.8 us (10%)
  other arithmetic  2.53 us (2%)
  between operations  1.39 us (1%)
    pallas_call x1, Pallas kernels, shards(): pl.pallas_call(functools.partial(body, nx, ny, nz), out_shape=(jax.ShapeD...  89.3 us
    unnamed x14, local copies, waits for them, and re-layouts  2.11 us

profile of v1, /device:TPU:14, one launch (start us, length us, event | category | flops | bytes accessed | tf_op | source)
XLA Modules:
  0.0 104.1 jit_solution(15971441668772808468)
XLA Ops:
  0.6 1.3 %slice_bitcast_fusion.1 = (bf16[1536,192]{0,1:T(8,128)(2,1)S(1)}, bf16[1536,192]{0,1:T(8,128)(2,1)S(1)}) fusion(bf16[1536,2,192]{0,2,1:T(8,128)(2,1)} %bitcast.69), kind=kLoop, calls=%fused_computation.2 | loop fusion | bytes 2359296 | tf_op jit(solution)/shard_map/squeeze | solution.py:402
  2.1 0.1 pad_maximum_fusion
  2.2 0.0 copy-start.1
  2.2 1.4 %copy.19 = bf16[1536,384]{1,0:T(8,128)(2,1)} copy(bf16[1536,384]{0,1:T(8,128)(2,1)S(1)} %pad_maximum_fusion) | data formatting | bytes 2359296 | tf_op jit(solution)/shard_map/concatenate | solution.py:403
  3.6 0.0 copy-done.1
  3.6 0.0 copy-start.4
  3.6 0.0 copy-start.5
  3.6 1.0 pad.9.owt_ref
  4.6 0.0 copy-done.2
  4.6 0.9 copy.21
  5.5 0.9 copy.18
  6.4 0.0 copy-done.5
  6.4 0.6 bitcast_bitcast_fusion.par_ref
  7.7 89.3 %conformer_backward.1 = (bf16[192,128]{1,0:T(8,128)(2,1)}, f32[3,24,128]{2,1,0:T(8,128)}, f32[2,24,128]{2,1,0:T(8,128)}, f32[2,32,128]{2,1,0:T(8,128)}, f32[8,128]{1,0:T(8,128)}) custom-call(s32[1]{0:T(128)S(6)} %copy.26.cnt_ref, bf16[128,1536]{1,0:T(8,128)(2,1)} %bitcast.65, bf16[8,192,128]{2,1,0:T(8,128)(2,1)} %bitcast.68, bf16[8,192,384]{2,1,0:T(8,128)(2,1)} %bitcast.64, ...), custom_call_target="tpu_custom_call" | custom-call | tf_op jit(solution)/shard_map/conformer_backward/pallas_call | solution.py:415
  97.1 0.8 slice_bitcast_fusion.5
  97.8 0.1 fusion.1
  98.0 0.6 copy.22
  98.6 0.8 slice_bitcast_fusion.10
  99.4 0.8 slice_bitcast_fusion.9
  100.1 0.6 pad_maximum_fusion.1
  100.7 0.6 maximum_bitcast_fusion.4
  101.3 0.7 slice_bitcast_fusion.3
  102.0 0.6 maximum_bitcast_fusion.1
  102.7 1.4 %copy.27 = bf16[1,1,128,192]{2,3,1,0:T(8,128)(2,1)} copy(bf16[1,1,128,192]{2,3,1,0:T(8,128)(2,1)} %bitcast.73) | data formatting | bytes 98304
  (13 shorter events, 0.1 us)
Async XLA Ops:
  2.2 1.4 %copy-start.1 = (bf16[1,1536,192]{1,2,0:T(8,128)(2,1)S(1)}, bf16[1,1536,192]{1,2,0:T(8,128)(2,1)}, u32[]{:S(2)}) copy-start(bf16[1,1536,192]{1,2,0:T(8,128)(2,1)} %param.15) | copy-start | bytes 1769476
  3.6 1.0 copy-start.2
  3.6 1.9 %copy-start = (bf16[1,1,128,1536]{3,2,1,0:T(8,128)(2,1)S(1)}, bf16[1,1,128,1536]{3,2,1,0:T(8,128)(2,1)}, u32[]{:S(2)}) copy-start(bf16[1,1,128,1536]{3,2,1,0:T(8,128)(2,1)} %param.8) | copy-start | bytes 1179652
  3.6 2.8 %copy-start.3 = (f32[1,32,192]{2,1,0:T(8,128)S(1)}, f32[1,32,192]{2,1,0:T(8,128)}, u32[]{:S(2)}) copy-start(f32[1,32,192]{2,1,0:T(8,128)} %param.12) | copy-start | bytes 73732
  3.6 2.8 %copy-start.4 = (f32[1,192]{1,0:T(1,128)S(1)}, f32[1,192]{1,0:T(1,128)}, u32[]{:S(2)}) copy-start(f32[1,192]{1,0:T(1,128)} %param.14) | copy-start | bytes 2308
  3.6 2.8 %copy-start.5 = (f32[1,192]{1,0:T(1,128)S(1)}, f32[1,192]{1,0:T(1,128)}, u32[]{:S(2)}) copy-start(f32[1,192]{1,0:T(1,128)} %param.13) | copy-start | bytes 2308

commit v2 on v1

v2 whole, which is shorter than its diff:
```python
import functools

import jax
import jax.numpy as jnp
from jax import lax
from jax.experimental import pallas as pl
from jax.experimental.pallas import tpu as pltpu
from jax.sharding import PartitionSpec as P

KERNEL = 32
EPSILON = 1e-05
FRAMES = 128
LANES = 128
NY = 8
PAD = 16

STAT_Y, STAT_Z, SUM_Y, SUM_Z, PART, GATHER = 0, 1, 2, 3, 4, 5
OUT_1, OUT_2, TAP_Z, TAP_Y = 6, 7, 8, 9
GLU_Y1, GLU_Z2, GLU_Z1, GLU_Y2 = 10, 11, 12, 13
TAIL_Y1, TAIL_Z2, TAIL_Z1, TAIL_Y2 = 14, 15, 16, 17
STAGES = 18
HALF = LANES // 2
MESH = pl.DeviceIdType.MESH
WIDE = (((1,), (1,)), ((), ()))


def body(
    nx, ny, nz, cnt_hbm, x_hbm, glu_hbm, taps_hbm, gain_hbm, shift_hbm, out_hbm, cot_hbm,
    ig_ref, gg_ref, og_ref, kg_ref, gb_ref,
    cnt, xs, glus, taps, gains, shifts, outs, cots,
    par, xt, glut, up, hs, gpad, gcpad, convs, normeds, dacts, acts, gas, gss, gps,
    st_y, st_z, su_y, su_z, rx, share,
    gs_y, gs_z, gs_t, gy1, gy1s, gz2, gz1, gz1s, gy2, ty1, ty1s, tz2, tz1, tz1s, ty2,
    osend, oy1, oy1s, oz2, kz, ky, local_sem, send_sem, recv_sem,
):
    dp = lax.axis_index("dp")
    core = lax.axis_index("pipe")
    mx = lax.axis_index("tensor")
    my = lax.rem(dp, ny)
    mz = lax.div(dp, ny)
    depth = xs.shape[1]
    channels = depth // nx
    rows = depth // (ny * nz)
    slab = ny * rows
    even = lax.rem(mz, 2) == 0
    pending = []

    def at_x(i):
        return (dp, core, i)

    def at_y(i):
        return (mz * ny + i, core, mx)

    def at_z(i):
        return (i * ny + my, core, mx)

    axes = {"x": (mx, nx, at_x), "y": (my, ny, at_y), "z": (mz, nz, at_z)}

    def around(axis, step, only=None):
        me, n, _ = axes[axis]

        @pl.loop(1, n)
        def _(r):
            peer = lax.rem(me + r, n)
            if only is None:
                step(peer)
            else:
                pl.when(lax.rem(peer, 2) == only)(lambda: step(peer))

    def copy(stage, axis, peer, src, dst):
        me, _, where = axes[axis]
        return pltpu.make_async_remote_copy(
            src_ref=src(peer), dst_ref=dst(me),
            send_sem=send_sem.at[stage, peer], recv_sem=recv_sem.at[stage, me],
            device_id=where(peer), device_id_type=MESH,
        )

    def push(stage, axis, src, dst, only=None):
        around(axis, lambda p: copy(stage, axis, p, src, dst).start(), only)
        pending.append(
            lambda: around(axis, lambda p: copy(stage, axis, p, src, dst).wait_send(), only)
        )

    def take(stage, axis, dst):
        where = axes[axis][2]
        around(axis, lambda p: pltpu.make_async_remote_copy(
            src_ref=dst(p), dst_ref=dst(p),
            send_sem=send_sem.at[stage, p], recv_sem=recv_sem.at[stage, p],
            device_id=where(p), device_id_type=MESH,
        ).wait_recv())

    loads = [
        pltpu.make_async_copy(a, b, local_sem.at[i])
        for i, (a, b) in enumerate((
            (x_hbm, xs), (glu_hbm, glus), (taps_hbm, taps), (gain_hbm, gains),
            (shift_hbm, shifts), (cnt_hbm, cnt), (out_hbm, outs), (cot_hbm, cots),
        ))
    ]
    for load in loads:
        load.start()

    barrier = pltpu.get_barrier_semaphore()
    for axis in ("x", "y", "z"):
        where = axes[axis][2]
        around(axis, lambda p: pl.semaphore_signal(
            barrier, inc=1, device_id=where(p), device_id_type=MESH
        ))

    @pl.loop(0, nx)
    def _(i):
        pl.semaphore_signal(barrier, inc=1, device_id=(dp, 1 - core, i), device_id_type=MESH)

    zero_pad = jnp.zeros((PAD, LANES), jnp.float32)
    zero_half = jnp.zeros((FRAMES, HALF), jnp.float32)
    for j in range(2):
        for ref in (gpad, gcpad):
            ref[j, 0:PAD, :] = zero_pad
            ref[j, PAD + FRAMES :, :] = zero_pad
        hs[j, 1, :, HALF:] = zero_half
    gas[1, :, HALF:] = zero_half
    par[1] = jnp.zeros(par.shape[1:], jnp.float32)
    for load in loads[2:6]:
        load.wait()
    count = cnt[0]
    frame = lax.broadcasted_iota(jnp.int32, (FRAMES, LANES), 0)
    valid = (frame < count).astype(jnp.float32)
    for ref, at, size in ((taps, 0, KERNEL), (gains, KERNEL, 1), (shifts, KERNEL + 1, 1)):
        par[0, pl.ds(at, size), :] = ref[:, 0:LANES]
        par[1, pl.ds(at, size), 0:HALF] = ref[:, LANES:]

    for load in loads[0:2]:
        load.wait()
    for i in range(2):
        h = lax.dot_general(xs[...], glus[i], WIDE, preferred_element_type=jnp.float32)
        hs[i, 0] = h[:, 0:LANES]
        hs[i, 1, :, 0:HALF] = h[:, LANES:]
    for j in range(2):
        squash_b = jax.nn.sigmoid(hs[1, j])
        hs[1, j] = squash_b
        gpad[j, PAD : PAD + FRAMES, :] = hs[0, j] * squash_b * valid
    for j in range(2):
        acc = jnp.zeros((FRAMES, LANES), jnp.float32)
        for b in range(8):
            window = gpad[j, pl.ds(b, FRAMES + 24), :]
            for a in range(KERNEL // 8):
                acc = acc + par[j, pl.ds(8 * a + b, 1), :] * window[8 * a : 8 * a + FRAMES]
        convs[j] = acc
        masked = acc * valid
        st_y[my, pl.ds(j, 1), :] = jnp.sum(masked, axis=0, keepdims=True)
        st_y[my, pl.ds(2 + j, 1), :] = jnp.sum(masked * acc, axis=0, keepdims=True)
    st_y[my, pl.ds(4, 4), :] = jnp.full((4, LANES), count, jnp.int32).astype(jnp.float32)

    def summed(buf, n):
        total = buf[0]
        for s in range(1, n):
            total = total + buf[s]
        return total

    def slot(buf):
        return lambda i: buf.at[i]

    def flip(src, dst):
        @pl.loop(0, depth // LANES)
        def _(c):
            at = pl.multiple_of(c * LANES, LANES)
            dst[pl.ds(at, LANES), :] = jnp.transpose(src[:, pl.ds(at, LANES)])

    pl.semaphore_wait(barrier, (nx - 1) + (ny - 1) + (nz - 1) + nx)
    push(STAT_Y, "y", lambda i: st_y.at[my], slot(st_y))

    for load in loads[6:]:
        load.wait()

    @pl.when(core == 1)
    def _():
        ga = lax.dot_general(cots[...], outs[...], WIDE, preferred_element_type=jnp.float32)
        gas[0] = ga[:, 0:LANES]
        gas[1, :, 0:HALF] = ga[:, LANES:]

    take(STAT_Y, "y", slot(st_y))
    st_z[mz] = summed(st_y, ny)
    push(STAT_Z, "z", lambda i: st_z.at[mz], slot(st_z))

    @pl.loop(0, depth // LANES)
    def _(c):
        at = pl.multiple_of(c * LANES, LANES)
        glut[pl.ds(at, LANES), 0:LANES] = jnp.transpose(glus[0, 0:LANES, pl.ds(at, LANES)])
        glut[pl.ds(at, LANES), LANES : 2 * LANES] = jnp.transpose(glus[1, 0:LANES, pl.ds(at, LANES)])
        glut[pl.ds(at, LANES), 2 * LANES :] = jnp.transpose(
            jnp.concatenate([glus[0, LANES:, pl.ds(at, LANES)], glus[1, LANES:, pl.ds(at, LANES)]], axis=0)
        )

    take(STAT_Z, "z", slot(st_z))
    stats = summed(st_z, nz)
    total = stats[4:5]
    factors = []
    for j in range(2):
        gain = par[j, pl.ds(KERNEL, 1), :]
        shift = par[j, pl.ds(KERNEL + 1, 1), :]
        center = stats[j : j + 1] / total
        inv_std = lax.rsqrt(stats[2 + j : 3 + j] / total - center * center + EPSILON)
        factors.append(gain * inv_std)
        normed = (convs[j] - center) * inv_std
        scaled = gain * normed + shift
        squash = jax.nn.sigmoid(scaled)
        normeds[j] = normed
        dacts[j] = valid * squash * (1.0 + scaled * (1.0 - squash))
        acts[:, j * LANES : (j + 1) * LANES] = (scaled * squash * valid).astype(jnp.bfloat16)

    def block(i):
        return pl.ds(pl.multiple_of(i * channels, channels), channels)

    def gather_copy(i):
        return pltpu.make_async_remote_copy(
            src_ref=share, dst_ref=up.at[block(mx)],
            send_sem=send_sem.at[GATHER, i], recv_sem=recv_sem.at[GATHER, mx],
            device_id=(dp, 0, i), device_id_type=MESH,
        )

    @pl.when(core == 0)
    def _():
        flip(xs, xt)

        @pl.loop(0, nx)
        def _(i):
            pltpu.make_async_remote_copy(
                src_ref=share, dst_ref=up.at[block(i)],
                send_sem=send_sem.at[GATHER, 0], recv_sem=recv_sem.at[GATHER, i],
                device_id=(dp, 1, i), device_id_type=MESH,
            ).wait_recv()

        ga = jnp.dot(outs[...], up[...], preferred_element_type=jnp.float32)
        gas[0] = jnp.transpose(ga[0:LANES])
        gas[1, :, 0:HALF] = jnp.transpose(ga[LANES:])

    for j in range(2):
        gs = gas[j] * dacts[j]
        gss[j] = gs
        su_y[my, pl.ds(j, 1), :] = jnp.sum(gs, axis=0, keepdims=True)
        su_y[my, pl.ds(2 + j, 1), :] = jnp.sum(gs * normeds[j], axis=0, keepdims=True)
    su_y[my, pl.ds(4, 4), :] = jnp.zeros((4, LANES), jnp.float32)
    push(SUM_Y, "y", lambda i: su_y.at[my], slot(su_y))

    @pl.when(core == 1)
    def _():
        flip(xs, xt)
        flip(cots, up)

    take(SUM_Y, "y", slot(su_y))
    su_z[mz] = summed(su_y, ny)
    push(SUM_Z, "z", lambda i: su_z.at[mz], slot(su_z))

    @pl.loop(0, nz)
    def _(z):
        at = pl.ds(pl.multiple_of(z * slab, slab), slab)
        part = jnp.dot(up[at, :], acts[...], preferred_element_type=jnp.float32)
        for i in range(2):
            osend[i, z] = part[:, i * LANES : (i + 1) * LANES].reshape(ny, rows, LANES).astype(jnp.bfloat16)

    push(OUT_1, "y", lambda i: osend.at[:, :, i], slot(oy1))
    take(SUM_Z, "z", slot(su_z))
    sums = summed(su_z, nz)
    gb_ref[...] = sums
    for j in range(2):
        gcpad[j, PAD : PAD + FRAMES, :] = (
            factors[j]
            * (gss[j] - sums[j : j + 1] / total - normeds[j] * (sums[2 + j : 3 + j] / total))
            * valid
        )
    halves = []
    for j in range(2):
        acc = jnp.zeros((FRAMES, LANES), jnp.float32)
        for b in range(8):
            first = 1 if b == 0 else 0
            window = gcpad[j, pl.ds(b, FRAMES + 24 + 8 * first), :]
            for a in range(first, first + KERNEL // 8):
                k = KERNEL - 8 * a - b
                acc = acc + par[j, pl.ds(k, 1), :] * window[8 * a : 8 * a + FRAMES]
        gate = hs[1, j]
        gg = acc * valid * gate
        halves.append((gg, gg * hs[0, j] * (1.0 - gate)))
    gps[:, 0:LANES] = halves[0][0].astype(jnp.bfloat16)
    gps[:, LANES : 2 * LANES] = halves[0][1].astype(jnp.bfloat16)
    gps[:, 2 * LANES :] = (halves[1][0] + pltpu.roll(halves[1][1], HALF, 1)).astype(jnp.bfloat16)

    def partial_of(i):
        return lax.dot_general(
            glut[block(i), :], gps[...], WIDE, preferred_element_type=jnp.float32
        ).astype(jnp.bfloat16)

    def part_copy(i):
        return copy(PART, "x", i, lambda p: rx.at[1, p], lambda p: rx.at[0, p])

    def send_part(i):
        rx[1, i] = partial_of(i)
        part_copy(i).start()

    around("x", send_part)
    pending.append(lambda: around("x", lambda i: part_copy(i).wait_send()))
    rx[0, mx] = partial_of(mx)

    @pl.loop(0, nz)
    def _(z):
        at = pl.ds(pl.multiple_of(z * slab, slab), slab)
        part = jnp.dot(xt[at, :], gps[...], preferred_element_type=jnp.float32)
        for i, ref in enumerate((gs_y.at[z], gs_z.at[z], gs_t.at[lax.rem(z, 2), lax.div(z, 2)])):
            ref[...] = part[:, i * LANES : (i + 1) * LANES].reshape(ny, rows, LANES).astype(jnp.bfloat16)

    push(GLU_Z1, "z", lambda i: gs_z.at[i], slot(gz1))
    push(GLU_Y1, "y", lambda i: gs_y.at[:, i], slot(gy1))
    push(TAIL_Z1, "z", lambda i: gs_t.at[1, lax.div(i, 2)], slot(tz1), 1)
    push(TAIL_Y1, "y", lambda i: gs_t.at[0, :, i], slot(ty1))

    def input_grad():
        take(PART, "x", lambda s: rx.at[0, s])
        acc = rx[0, 0].astype(jnp.float32)
        for s in range(1, nx):
            acc = acc + rx[0, s].astype(jnp.float32)
        final = (up[block(mx), :].astype(jnp.float32) + acc).astype(jnp.bfloat16)
        share[...] = final
        ig_ref[...] = final

    @pl.when(core == 1)
    def _():
        input_grad()

        @pl.loop(0, nx)
        def _(i):
            gather_copy(i).start()

    for j in range(2):
        gc = gcpad[j, PAD : PAD + FRAMES, :]
        for b in range(8):
            window = gpad[j, pl.ds(b, FRAMES + 24), :]
            for a in range(KERNEL // 8):
                kz[mz, j, pl.ds(8 * a + b, 1), :] = jnp.sum(
                    gc * window[8 * a : 8 * a + FRAMES], axis=0, keepdims=True
                )
    push(TAP_Z, "z", lambda i: kz.at[mz], slot(kz))

    def reduced(stage, axis, buf, own):
        take(stage, axis, slot(buf))
        me, n, _ = axes[axis]
        acc = own.astype(jnp.float32)
        for r in range(1, n):
            acc = acc + buf[lax.rem(me + r, n)].astype(jnp.float32)
        return acc

    oy1s[...] = reduced(OUT_1, "y", oy1, osend[:, :, my]).astype(jnp.bfloat16)
    push(OUT_2, "z", lambda i: oy1s.at[:, i], slot(oz2))

    @pl.when(core == 0)
    def _():
        input_grad()

    take(TAP_Z, "z", slot(kz))
    ky[my] = summed(kz, nz)
    push(TAP_Y, "y", lambda i: ky.at[my], slot(ky))

    gz1s[...] = reduced(GLU_Z1, "z", gz1, gs_z[mz]).astype(jnp.bfloat16)
    push(GLU_Y2, "y", slot(gz1s), slot(gy2))
    gy1s[...] = reduced(GLU_Y1, "y", gy1, gs_y[:, my]).astype(jnp.bfloat16)
    push(GLU_Z2, "z", slot(gy1s), slot(gz2))

    @pl.when(jnp.logical_not(even))
    def _():
        tz1s[...] = reduced(TAIL_Z1, "z", tz1, gs_t[1, lax.div(mz, 2)]).astype(jnp.bfloat16)
        around("y", lambda p: copy(TAIL_Y2, "y", p, slot(tz1s), slot(ty2)).start())

    ty1s[...] = reduced(TAIL_Y1, "y", ty1, gs_t[0, :, my]).astype(jnp.bfloat16)
    push(TAIL_Z2, "z", lambda i: ty1s.at[lax.div(i, 2)], slot(tz2), 0)

    og_ref[...] = reduced(OUT_2, "z", oz2, oy1s[:, mz])
    take(TAP_Y, "y", slot(ky))
    kg_ref[...] = summed(ky, ny)
    gg_ref[1] = reduced(GLU_Y2, "y", gy2, gz1s[my])
    gg_ref[0] = reduced(GLU_Z2, "z", gz2, gy1s[mz])

    @pl.when(jnp.logical_not(even))
    def _():
        gg_ref[2] = reduced(TAIL_Y2, "y", ty2, tz1s[my])
        around("y", lambda p: copy(TAIL_Y2, "y", p, slot(tz1s), slot(ty2)).wait_send())

    @pl.when(even)
    def _():
        gg_ref[2] = reduced(TAIL_Z2, "z", tz2, ty1s[lax.div(mz, 2)])

    for wait in pending:
        wait()

    @pl.when(core == 1)
    def _():
        @pl.loop(0, nx)
        def _(i):
            gather_copy(i).wait_send()


def unpack(gg, og, kg, gb, ig, ig_out, glu_out, out_out, taps_out, gain_out, bias_out):
    ig_out[...] = ig[...]
    for i in range(2):
        glu_out[:, i, 0:LANES] = gg[i]
        glu_out[:, i, LANES:] = gg[2, :, i * HALF : (i + 1) * HALF]
    out_out[:, 0:LANES] = og[0]
    out_out[:, LANES:] = og[1, :, 0:HALF]
    taps_out[:, 0:LANES] = kg[0]
    taps_out[:, LANES:] = kg[1, :, 0:HALF]
    for ref, at in ((bias_out, 0), (gain_out, 2)):
        ref[:, 0:LANES] = gb[at : at + 1, :]
        ref[:, LANES:] = gb[at + 1 : at + 2, 0:HALF]


def shards(
    ny, saved_inputs, cotangent, frame_counts, glu_weight, conv_kernel, norm_gain, norm_bias, out_weight
):
    nx = lax.axis_size("tensor")
    nz = lax.axis_size("dp") // ny
    depth = saved_inputs.shape[-1]
    channels = depth // nx
    rows = depth // (ny * nz)

    f32, bf16 = jnp.float32, jnp.bfloat16
    operands = (
        frame_counts,
        saved_inputs[0, 0],
        glu_weight[0].transpose(1, 2, 0),
        conv_kernel[0],
        norm_gain,
        norm_bias,
        out_weight[0].T,
        cotangent[0],
    )
    vmem = pl.BlockSpec(memory_space=pltpu.VMEM)
    big = pltpu.VMEM((2, FRAMES, LANES), f32)
    padded = pltpu.VMEM((2, FRAMES + 2 * PAD, LANES), f32)

    def wire(*shape):
        return pltpu.VMEM(shape + (rows, LANES), bf16)

    sem = pltpu.SemaphoreType.DMA((STAGES, max(nx, ny, nz)))
    ig, gg, og, kg, gb = pl.pallas_call(
        functools.partial(body, nx, ny, nz),
        out_shape=(
            jax.ShapeDtypeStruct((channels, FRAMES), bf16),
            jax.ShapeDtypeStruct((3, rows, LANES), f32),
            jax.ShapeDtypeStruct((2, rows, LANES), f32),
            jax.ShapeDtypeStruct((2, KERNEL, LANES), f32),
            jax.ShapeDtypeStruct((8, LANES), f32),
        ),
        in_specs=[pl.BlockSpec(memory_space=pl.ANY)] * len(operands),
        out_specs=(vmem,) * 5,
        scratch_shapes=[
            pltpu.SMEM((1,), jnp.int32),
            *(pltpu.VMEM(a.shape, a.dtype) for a in operands[1:]),
            pltpu.VMEM((2, KERNEL + 8, LANES), f32),
            pltpu.VMEM((depth, FRAMES), bf16),
            pltpu.VMEM((depth, 3 * LANES), bf16),
            pltpu.VMEM((depth, FRAMES), bf16),
            pltpu.VMEM((2, 2, FRAMES, LANES), f32),
            padded, padded,
            big, big, big,
            pltpu.VMEM((FRAMES, 2 * LANES), bf16),
            big, big,
            pltpu.VMEM((FRAMES, 3 * LANES), bf16),
            *(pltpu.VMEM((n, 8, LANES), f32) for n in (ny, nz, ny, nz)),
            pltpu.VMEM((2, nx, channels, FRAMES), bf16),
            pltpu.VMEM((channels, FRAMES), bf16),
            wire(nz, ny), wire(nz, ny), wire(2, nz // 2, ny),
            wire(ny, nz), wire(nz), wire(nz), wire(nz, ny), wire(ny), wire(ny),
            wire(ny, nz // 2), wire(nz // 2), wire(nz), wire(nz, ny), wire(ny), wire(ny),
            wire(2, nz, ny), wire(ny, 2, nz), wire(2, nz), wire(nz, 2),
            pltpu.VMEM((nz, 2, KERNEL, LANES), f32),
            pltpu.VMEM((ny, 2, KERNEL, LANES), f32),
            pltpu.SemaphoreType.DMA((len(operands),)),
            sem, sem,
        ],
        compiler_params=pltpu.CompilerParams(collective_id=0, has_side_effects=True),
        name="conformer_backward",
    )(*operands)
    ig, glu, out, taps, gain, bias = pl.pallas_call(
        unpack,
        out_shape=(
            jax.ShapeDtypeStruct((channels, FRAMES), bf16),
            jax.ShapeDtypeStruct((rows, 2, channels), f32),
            jax.ShapeDtypeStruct((rows, channels), f32),
            jax.ShapeDtypeStruct((KERNEL, channels), f32),
            jax.ShapeDtypeStruct((1, channels), f32),
            jax.ShapeDtypeStruct((1, channels), f32),
        ),
        in_specs=[vmem] * 5,
        out_specs=(vmem,) * 6,
        name="unpack",
    )(gg, og, kg, gb, ig)
    return (ig.T[None, None], glu[None], out[None], taps[None], gain, bias)


def solution(mesh):
    placed = (
        P("pipe", "dp", None, None),
        P("dp", None, None),
        P("dp"),
        P("pipe", None, None, "tensor"),
        P("pipe", None, "tensor"),
        P("pipe", "tensor"),
        P("pipe", "tensor"),
        P("pipe", None, "tensor"),
    )
    return jax.shard_map(
        functools.partial(shards, NY),
        mesh=mesh,
        in_specs=placed,
        out_specs=(
            P("pipe", "dp", None, "tensor"),
            P("pipe", "dp", None, "tensor"),
            P("pipe", "dp", "tensor"),
            P("pipe", None, "tensor"),
            P("pipe", "tensor"),
            P("pipe", "tensor"),
        ),
        check_vma=False,
    )
```

time: 105 us -> 95.6 us (0.910)
  local copies, waits for them, and re-layouts: 10.8 us -> 0 us
  Pallas kernels: 89.3 us -> 92.8 us
  other arithmetic: 2.53 us -> 0 us
    squeeze x4 -> x0, local copies, waits for them, and re-layouts: 3.6 us -> none  [the longest x1 1.32 us: shards(): first, second = (glu[:, 0], glu[:, 1])]
    unnamed x14 -> x0, local copies, waits for them, and re-layouts: 2.11 us -> none
    pallas_call x1, Pallas kernels: 89.3 us -> 91.2 us  [shards(): pl.pallas_call(functools.partial(body, nx, ny, nz), out_shape=(jax.ShapeD...]
    transpose x2 -> x0, local copies, waits for them, and re-layouts: 1.83 us -> none  [the longest x1 0.92 us: shards(): cot_t = cotangent[0].T.reshape(nx, channels, FRAMES)]
    pallas_call x0 -> x1, Pallas kernels: none -> 1.59 us  [shards(): pl.pallas_call(unpack, out_shape=(jax.ShapeDtypeStruct((channels, FRAMES)...]
    concatenate x1 -> x0, local copies, waits for them, and re-layouts: 1.41 us -> none  [shards(): jnp.concatenate([first[:, :LANES], second[:, :LANES], first[:, LANES:], s...]
    broadcast_in_dim x3 -> x0, other arithmetic: 1.24 us -> none  [the longest x1 0.62 us: shards(): kernel_grad = jnp.concatenate([kg[0], kg[1][:, :half]], axis=1)[None]]
where the time goes in v2:
time: 95.6 us; the launch traced here: 94.1 us
  Pallas kernels  92.8 us (97%)
  between operations  1.29 us (1%)
    pallas_call x1, Pallas kernels, shards(): pl.pallas_call(functools.partial(body, nx, ny, nz), out_shape=(jax.ShapeD...  91.2 us

profile of v2, /device:TPU:14, one launch (start us, length us, event | category | flops | bytes accessed | tf_op | source)
XLA Modules:
  0.0 94.1 jit_solution(2420728630776651458)
XLA Ops:
  1.3 91.2 %conformer_backward.1 = (bf16[192,128]{1,0:T(8,128)(2,1)}, f32[3,24,128]{2,1,0:T(8,128)}, f32[2,24,128]{2,1,0:T(8,128)}, f32[2,32,128]{2,1,0:T(8,128)}, f32[8,128]{1,0:T(8,128)}) custom-call(s32[1]{0:T(128)S(6)} %copy.14.cnt_hbm, bf16[128,1536]{1,0:T(8,128)(2,1)} %bitcast.17, bf16[2,192,1536]{2,1,0:T(8,128)(2,1)} %bitcast.15, f32[32,192]{1,0:T(8,128)} %bitcast.19, ...), custom_call_target="tpu_custom_call" | custom-call | tf_op jit(solution)/shard_map/conformer_backward/pallas_call | solution.py:440
  92.5 1.6 %unpack.1 = (bf16[192,128]{1,0:T(8,128)(2,1)}, f32[24,2,192]{2,1,0:T(2,128)}, f32[24,192]{1,0:T(8,128)}, f32[32,192]{1,0:T(8,128)}, f32[1,192]{1,0:T(1,128)}, /*index=5*/f32[1,192]{1,0:T(1,128)}) custom-call(f32[3,24,128]{2,1,0:T(8,128)} %get-tuple-element.17.gg, f32[2,24,128]{2,1,0:T(8,128)} %get-tuple-element.18.og, f32[2,32,128]{2,1,0:T(8,128)} %get-tuple-element.19.kg, ...), custom_call_target="tpu_custom_call" | custom-call | tf_op jit(solution)/shard_map/unpack/pallas_call | solution.py:479

commit v3 on v2

--- a/solution.py
+++ b/solution.py
@@ -15,10 +15,10 @@
 PAD = 16
 
 STAT_Y, STAT_Z, SUM_Y, SUM_Z, PART, GATHER = 0, 1, 2, 3, 4, 5
-OUT_1, OUT_2, TAP_Z, TAP_Y = 6, 7, 8, 9
-GLU_Y1, GLU_Z2, GLU_Z1, GLU_Y2 = 10, 11, 12, 13
-TAIL_Y1, TAIL_Z2, TAIL_Z1, TAIL_Y2 = 14, 15, 16, 17
-STAGES = 18
+OUT_Y1, OUT_Z2, OUT_Z1, OUT_Y2 = 6, 7, 8, 9
+TAP_Z1, TAP_Y, TAP_Z2 = 10, 11, 12
+IN_Y, IN_Z, PROJ_Y, PROJ_Z, GLU_Z2, GLU_Y2 = 13, 14, 15, 16, 17, 18
+STAGES = 19
 HALF = LANES // 2
 MESH = pl.DeviceIdType.MESH
 WIDE = (((1,), (1,)), ((), ()))
@@ -30,8 +30,8 @@
     cnt, xs, glus, taps, gains, shifts, outs, cots,
     par, xt, glut, up, hs, gpad, gcpad, convs, normeds, dacts, acts, gas, gss, gps,
     st_y, st_z, su_y, su_z, rx, share,
-    gs_y, gs_z, gs_t, gy1, gy1s, gz2, gz1, gz1s, gy2, ty1, ty1s, tz2, tz1, tz1s, ty2,
-    osend, oy1, oy1s, oz2, kz, ky, local_sem, send_sem, recv_sem,
+    xw, xy, xz, xl, gp, py, pz, prod, gz1, gz2, gy1, gy2,
+    osend, oy1, oy1s, oz2, oz1, oz1s, oy2, ks, kz, ky, kg, local_sem, send_sem, recv_sem,
 ):
     dp = lax.axis_index("dp")
     core = lax.axis_index("pipe")
@@ -42,7 +42,6 @@
     channels = depth // nx
     rows = depth // (ny * nz)
     slab = ny * rows
-    even = lax.rem(mz, 2) == 0
     pending = []
 
     def at_x(i):
@@ -56,16 +55,13 @@
 
     axes = {"x": (mx, nx, at_x), "y": (my, ny, at_y), "z": (mz, nz, at_z)}
 
-    def around(axis, step, only=None):
+    def around(axis, step):
         me, n, _ = axes[axis]
 
         @pl.loop(1, n)
-        def _(r):
-            peer = lax.rem(me + r, n)
-            if only is None:
-                step(peer)
-            else:
-                pl.when(lax.rem(peer, 2) == only)(lambda: step(peer))
+        def _(i):
+            off = lax.div(i, 2)
+            step(lax.rem(me + n // 2 + jnp.where(lax.rem(i, 2) == 0, off, n - off), n))
 
     def copy(stage, axis, peer, src, dst):
         me, _, where = axes[axis]
@@ -75,11 +71,14 @@
             device_id=where(peer), device_id_type=MESH,
         )
 
-    def push(stage, axis, src, dst, only=None):
-        around(axis, lambda p: copy(stage, axis, p, src, dst).start(), only)
-        pending.append(
-            lambda: around(axis, lambda p: copy(stage, axis, p, src, dst).wait_send(), only)
-        )
+    def push(stage, axis, src, dst, now=True):
+        def start():
+            around(axis, lambda p: copy(stage, axis, p, src, dst).start())
+
+        pending.append(lambda: around(axis, lambda p: copy(stage, axis, p, src, dst).wait_send()))
+        if now:
+            start()
+        return start
 
     def take(stage, axis, dst):
         where = axes[axis][2]
@@ -165,6 +164,34 @@
             at = pl.multiple_of(c * LANES, LANES)
             dst[pl.ds(at, LANES), :] = jnp.transpose(src[:, pl.ds(at, LANES)])
 
+    def send_inputs():
+        flip(xs, xt)
+
+        @pl.loop(0, nz)
+        def _(z):
+            part = xt[pl.ds(pl.multiple_of(z * slab, slab), slab), :].astype(jnp.float32)
+            xw[z] = part.reshape(ny, rows, LANES).astype(jnp.bfloat16)
+
+        start_y()
+        start_z()
+
+    def slab_of(i):
+        return pl.ds(pl.multiple_of(i * slab, slab), slab)
+
+    start_y = push(IN_Y, "y", lambda i: xw.at[:, i], slot(xy), False)
+    start_z = push(IN_Z, "z", lambda i: xt.at[slab_of(i)], slot(xz), False)
+
+    def place_inputs():
+        take(IN_Y, "y", slot(xy))
+        take(IN_Z, "z", slot(xz))
+        xy[my] = xw[:, my]
+        xz[mz] = xt[slab_of(mz), :]
+        for i in range(ny):
+            part = xy[i].astype(jnp.float32).reshape(nz * rows, LANES)
+            xl[0, 0 : nz * rows, i * LANES : (i + 1) * LANES] = part.astype(jnp.bfloat16)
+        for i in range(nz):
+            xl[1, :, i * LANES : (i + 1) * LANES] = xz[i]
+
     pl.semaphore_wait(barrier, (nx - 1) + (ny - 1) + (nz - 1) + nx)
     push(STAT_Y, "y", lambda i: st_y.at[my], slot(st_y))
 
@@ -219,17 +246,18 @@
 
     @pl.when(core == 0)
     def _():
-        flip(xs, xt)
-
-        @pl.loop(0, nx)
-        def _(i):
-            pltpu.make_async_remote_copy(
-                src_ref=share, dst_ref=up.at[block(i)],
-                send_sem=send_sem.at[GATHER, 0], recv_sem=recv_sem.at[GATHER, i],
-                device_id=(dp, 1, i), device_id_type=MESH,
-            ).wait_recv()
-
-        ga = jnp.dot(outs[...], up[...], preferred_element_type=jnp.float32)
+        send_inputs()
+        place_inputs()
+        ga = jnp.zeros((channels, FRAMES), jnp.float32)
+        for i in range(0, nx, 2):
+            for k in (i, i + 1):
+                pltpu.make_async_remote_copy(
+                    src_ref=share, dst_ref=up.at[k * channels : (k + 1) * channels],
+                    send_sem=send_sem.at[GATHER, 0], recv_sem=recv_sem.at[GATHER, k],
+                    device_id=(dp, 1, k), device_id_type=MESH,
+                ).wait_recv()
+            pair = slice(i * channels, (i + 2) * channels)
+            ga = ga + jnp.dot(outs[:, pair], up[pair, :], preferred_element_type=jnp.float32)
         gas[0] = jnp.transpose(ga[0:LANES])
         gas[1, :, 0:HALF] = jnp.transpose(ga[LANES:])
 
@@ -243,7 +271,6 @@
 
     @pl.when(core == 1)
     def _():
-        flip(xs, xt)
         flip(cots, up)
 
     take(SUM_Y, "y", slot(su_y))
@@ -257,7 +284,13 @@
         for i in range(2):
             osend[i, z] = part[:, i * LANES : (i + 1) * LANES].reshape(ny, rows, LANES).astype(jnp.bfloat16)
 
-    push(OUT_1, "y", lambda i: osend.at[:, :, i], slot(oy1))
+    push(OUT_Y1, "y", lambda i: osend.at[0, :, i], slot(oy1))
+    push(OUT_Z1, "z", lambda i: osend.at[1, i], slot(oz1))
+
+    @pl.when(core == 1)
+    def _():
+        send_inputs()
+
     take(SUM_Z, "z", slot(su_z))
     sums = summed(su_z, nz)
     gb_ref[...] = sums
@@ -283,6 +316,19 @@
     gps[:, LANES : 2 * LANES] = halves[0][1].astype(jnp.bfloat16)
     gps[:, 2 * LANES :] = (halves[1][0] + pltpu.roll(halves[1][1], HALF, 1)).astype(jnp.bfloat16)
 
+    for i, wide in enumerate(((halves[0][0], halves[1][0]), (halves[0][1], halves[1][1]))):
+        gp[i, 0:FRAMES, :] = wide[0].astype(jnp.bfloat16)
+        gp[i, FRAMES:, :] = (
+            wide[1][0 : FRAMES // 2] + pltpu.roll(wide[1][FRAMES // 2 :], HALF, 1)
+        ).astype(jnp.bfloat16)
+    proj_y = push(PROJ_Y, "y", lambda i: gp.at[0], slot(py), False)
+    proj_z = push(PROJ_Z, "z", lambda i: gp.at[1], slot(pz), False)
+
+    @pl.when(core == 0)
+    def _():
+        proj_y()
+        proj_z()
+
     def partial_of(i):
         return lax.dot_general(
             glut[block(i), :], gps[...], WIDE, preferred_element_type=jnp.float32
@@ -299,17 +345,11 @@
     pending.append(lambda: around("x", lambda i: part_copy(i).wait_send()))
     rx[0, mx] = partial_of(mx)
 
-    @pl.loop(0, nz)
-    def _(z):
-        at = pl.ds(pl.multiple_of(z * slab, slab), slab)
-        part = jnp.dot(xt[at, :], gps[...], preferred_element_type=jnp.float32)
-        for i, ref in enumerate((gs_y.at[z], gs_z.at[z], gs_t.at[lax.rem(z, 2), lax.div(z, 2)])):
-            ref[...] = part[:, i * LANES : (i + 1) * LANES].reshape(ny, rows, LANES).astype(jnp.bfloat16)
-
-    push(GLU_Z1, "z", lambda i: gs_z.at[i], slot(gz1))
-    push(GLU_Y1, "y", lambda i: gs_y.at[:, i], slot(gy1))
-    push(TAIL_Z1, "z", lambda i: gs_t.at[1, lax.div(i, 2)], slot(tz1), 1)
-    push(TAIL_Y1, "y", lambda i: gs_t.at[0, :, i], slot(ty1))
+    @pl.when(core == 1)
+    def _():
+        proj_y()
+        proj_z()
+
 
     def input_grad():
         take(PART, "x", lambda s: rx.at[0, s])
@@ -328,15 +368,19 @@
         def _(i):
             gather_copy(i).start()
 
+        place_inputs()
+
     for j in range(2):
         gc = gcpad[j, PAD : PAD + FRAMES, :]
         for b in range(8):
             window = gpad[j, pl.ds(b, FRAMES + 24), :]
             for a in range(KERNEL // 8):
-                kz[mz, j, pl.ds(8 * a + b, 1), :] = jnp.sum(
+                k, each = 8 * a + b, KERNEL // nz
+                ks[k // each, j, pl.ds(k % each, 1), :] = jnp.sum(
                     gc * window[8 * a : 8 * a + FRAMES], axis=0, keepdims=True
                 )
-    push(TAP_Z, "z", lambda i: kz.at[mz], slot(kz))
+    push(TAP_Z1, "z", slot(ks), slot(kz))
+    kz[mz] = ks[mz]
 
     def reduced(stage, axis, buf, own):
         take(stage, axis, slot(buf))
@@ -346,44 +390,51 @@
             acc = acc + buf[lax.rem(me + r, n)].astype(jnp.float32)
         return acc
 
-    oy1s[...] = reduced(OUT_1, "y", oy1, osend[:, :, my]).astype(jnp.bfloat16)
-    push(OUT_2, "z", lambda i: oy1s.at[:, i], slot(oz2))
+    oy1s[...] = reduced(OUT_Y1, "y", oy1, osend[0, :, my]).astype(jnp.bfloat16)
+    push(OUT_Z2, "z", slot(oy1s), slot(oz2))
+    oz1s[...] = reduced(OUT_Z1, "z", oz1, osend[1, mz]).astype(jnp.bfloat16)
+    push(OUT_Y2, "y", slot(oz1s), slot(oy2))
 
     @pl.when(core == 0)
     def _():
         input_grad()
 
-    take(TAP_Z, "z", slot(kz))
+    take(TAP_Z1, "z", slot(kz))
     ky[my] = summed(kz, nz)
     push(TAP_Y, "y", lambda i: ky.at[my], slot(ky))
 
-    gz1s[...] = reduced(GLU_Z1, "z", gz1, gs_z[mz]).astype(jnp.bfloat16)
-    push(GLU_Y2, "y", slot(gz1s), slot(gy2))
-    gy1s[...] = reduced(GLU_Y1, "y", gy1, gs_y[:, my]).astype(jnp.bfloat16)
-    push(GLU_Z2, "z", slot(gy1s), slot(gz2))
-
-    @pl.when(jnp.logical_not(even))
-    def _():
-        tz1s[...] = reduced(TAIL_Z1, "z", tz1, gs_t[1, lax.div(mz, 2)]).astype(jnp.bfloat16)
-        around("y", lambda p: copy(TAIL_Y2, "y", p, slot(tz1s), slot(ty2)).start())
-
-    ty1s[...] = reduced(TAIL_Y1, "y", ty1, gs_t[0, :, my]).astype(jnp.bfloat16)
-    push(TAIL_Z2, "z", lambda i: ty1s.at[lax.div(i, 2)], slot(tz2), 0)
-
-    og_ref[...] = reduced(OUT_2, "z", oz2, oy1s[:, mz])
+    low = lax.broadcasted_iota(jnp.int32, (FRAMES // 2, LANES), 1) < HALF
+
+    def products(i, stage, axis, buf, out):
+        take(stage, axis, slot(buf))
+        me, n, _ = axes[axis]
+        buf[me] = gp[i]
+        for k in range(n):
+            at = k * FRAMES
+            prod[i, at : at + FRAMES, 0:LANES] = buf[k, 0:FRAMES, :]
+            tail = buf[k, FRAMES:, :].astype(jnp.float32)
+            prod[i, at : at + FRAMES // 2, LANES:] = jnp.where(low, tail, 0.0).astype(jnp.bfloat16)
+            prod[i, at + FRAMES // 2 : at + FRAMES, LANES:] = jnp.where(
+                low, pltpu.roll(tail, HALF, 1), 0.0
+            ).astype(jnp.bfloat16)
+        total = jnp.dot(xl[i, :, 0 : n * FRAMES], prod[i, 0 : n * FRAMES], preferred_element_type=jnp.float32)
+        for k in range(2):
+            out[:, k] = total[:, k * LANES : (k + 1) * LANES].reshape(-1, rows, LANES).astype(jnp.bfloat16)
+
+    products(1, PROJ_Z, "z", pz, gz1)
+    push(GLU_Y2, "y", slot(gz1), slot(gy2))
+    products(0, PROJ_Y, "y", py, gy1)
+    push(GLU_Z2, "z", slot(gy1), slot(gz2))
     take(TAP_Y, "y", slot(ky))
-    kg_ref[...] = summed(ky, ny)
-    gg_ref[1] = reduced(GLU_Y2, "y", gy2, gz1s[my])
-    gg_ref[0] = reduced(GLU_Z2, "z", gz2, gy1s[mz])
-
-    @pl.when(jnp.logical_not(even))
-    def _():
-        gg_ref[2] = reduced(TAIL_Y2, "y", ty2, tz1s[my])
-        around("y", lambda p: copy(TAIL_Y2, "y", p, slot(tz1s), slot(ty2)).wait_send())
-
-    @pl.when(even)
-    def _():
-        gg_ref[2] = reduced(TAIL_Z2, "z", tz2, ty1s[lax.div(mz, 2)])
+    kg[mz] = summed(ky, ny)
+    push(TAP_Z2, "z", lambda i: kg.at[mz], slot(kg))
+
+    og_ref[0] = reduced(OUT_Z2, "z", oz2, oy1s[mz])
+    og_ref[1] = reduced(OUT_Y2, "y", oy2, oz1s[my])
+    gg_ref[1] = reduced(GLU_Y2, "y", gy2, gz1[my])
+    gg_ref[0] = reduced(GLU_Z2, "z", gz2, gy1[mz])
+    take(TAP_Z2, "z", slot(kg))
+    kg_ref[...] = kg[...]
 
     for wait in pending:
         wait()
@@ -398,12 +449,14 @@
 def unpack(gg, og, kg, gb, ig, ig_out, glu_out, out_out, taps_out, gain_out, bias_out):
     ig_out[...] = ig[...]
     for i in range(2):
-        glu_out[:, i, 0:LANES] = gg[i]
-        glu_out[:, i, LANES:] = gg[2, :, i * HALF : (i + 1) * HALF]
+        glu_out[:, i, 0:LANES] = gg[i, 0]
+        glu_out[:, i, LANES:] = gg[i, 1, :, 0:HALF]
     out_out[:, 0:LANES] = og[0]
     out_out[:, LANES:] = og[1, :, 0:HALF]
-    taps_out[:, 0:LANES] = kg[0]
-    taps_out[:, LANES:] = kg[1, :, 0:HALF]
+    for i in range(kg.shape[0]):
+        at = pl.ds(i * kg.shape[2], kg.shape[2])
+        taps_out[at, 0:LANES] = kg[i, 0]
+        taps_out[at, LANES:] = kg[i, 1, :, 0:HALF]
     for ref, at in ((bias_out, 0), (gain_out, 2)):
         ref[:, 0:LANES] = gb[at : at + 1, :]
         ref[:, LANES:] = gb[at + 1 : at + 2, 0:HALF]
@@ -441,9 +494,9 @@
         functools.partial(body, nx, ny, nz),
         out_shape=(
             jax.ShapeDtypeStruct((channels, FRAMES), bf16),
-            jax.ShapeDtypeStruct((3, rows, LANES), f32),
+            jax.ShapeDtypeStruct((2, 2, rows, LANES), f32),
             jax.ShapeDtypeStruct((2, rows, LANES), f32),
-            jax.ShapeDtypeStruct((2, KERNEL, LANES), f32),
+            jax.ShapeDtypeStruct((nz, 2, KERNEL // nz, LANES), f32),
             jax.ShapeDtypeStruct((8, LANES), f32),
         ),
         in_specs=[pl.BlockSpec(memory_space=pl.ANY)] * len(operands),
@@ -464,12 +517,20 @@
             *(pltpu.VMEM((n, 8, LANES), f32) for n in (ny, nz, ny, nz)),
             pltpu.VMEM((2, nx, channels, FRAMES), bf16),
             pltpu.VMEM((channels, FRAMES), bf16),
-            wire(nz, ny), wire(nz, ny), wire(2, nz // 2, ny),
+            wire(nz, ny), wire(ny, nz),
+            pltpu.VMEM((nz, ny * rows, LANES), bf16),
+            pltpu.VMEM((2, max(ny, nz) * rows, max(ny, nz) * LANES), bf16),
+            pltpu.VMEM((2, FRAMES + FRAMES // 2, LANES), bf16),
+            pltpu.VMEM((ny, FRAMES + FRAMES // 2, LANES), bf16),
+            pltpu.VMEM((nz, FRAMES + FRAMES // 2, LANES), bf16),
+            pltpu.VMEM((2, max(ny, nz) * FRAMES, 2 * LANES), bf16),
+            wire(ny, 2), wire(nz, 2), wire(nz, 2), wire(ny, 2),
+            wire(2, nz, ny),
             wire(ny, nz), wire(nz), wire(nz), wire(nz, ny), wire(ny), wire(ny),
-            wire(ny, nz // 2), wire(nz // 2), wire(nz), wire(nz, ny), wire(ny), wire(ny),
-            wire(2, nz, ny), wire(ny, 2, nz), wire(2, nz), wire(nz, 2),
-            pltpu.VMEM((nz, 2, KERNEL, LANES), f32),
-            pltpu.VMEM((ny, 2, KERNEL, LANES), f32),
+            pltpu.VMEM((nz, 2, KERNEL // nz, LANES), f32),
+            pltpu.VMEM((nz, 2, KERNEL // nz, LANES), f32),
+            pltpu.VMEM((ny, 2, KERNEL // nz, LANES), f32),
+            pltpu.VMEM((nz, 2, KERNEL // nz, LANES), f32),
             pltpu.SemaphoreType.DMA((len(operands),)),
             sem, sem,
         ],

time: 95.6 us -> 89.2 us (0.933); the launches traced: 94.1 us -> 89 us
  Pallas kernels: 92.8 us -> 87.7 us
    pallas_call x1, Pallas kernels: 91.2 us -> 86.2 us  [shards(): pl.pallas_call(functools.partial(body, nx, ny, nz), out_shape=(jax.ShapeD...]
where the time goes in v3:
time: 89.2 us; the launch traced here: 89 us
  Pallas kernels  87.7 us (98%)
  between operations  1.29 us (1%)
    pallas_call x1, Pallas kernels, shards(): pl.pallas_call(functools.partial(body, nx, ny, nz), out_shape=(jax.ShapeD...  86.2 us

profile of v3, /device:TPU:14, one launch (start us, length us, event | category | flops | bytes accessed | tf_op | source)
XLA Modules:
  0.0 89.0 jit_solution(4069425390976587784)
XLA Ops:
  1.3 86.2 %conformer_backward.1 = (bf16[192,128]{1,0:T(8,128)(2,1)}, f32[2,2,24,128]{3,2,1,0:T(8,128)}, f32[2,24,128]{2,1,0:T(8,128)}, f32[8,2,4,128]{3,2,1,0:T(4,128)}, f32[8,128]{1,0:T(8,128)}) custom-call(s32[1]{0:T(128)S(6)} %copy.14.cnt_hbm, bf16[128,1536]{1,0:T(8,128)(2,1)} %bitcast.17, bf16[2,192,1536]{2,1,0:T(8,128)(2,1)} %bitcast.15, f32[32,192]{1,0:T(8,128)} %bitcast.19, ...), custom_call_target="tpu_custom_call" | custom-call | tf_op jit(solution)/shard_map/conformer_backward/pallas_call | solution.py:493
  87.5 1.5 %unpack.1 = (bf16[192,128]{1,0:T(8,128)(2,1)}, f32[24,2,192]{2,1,0:T(2,128)}, f32[24,192]{1,0:T(8,128)}, f32[32,192]{1,0:T(8,128)}, f32[1,192]{1,0:T(1,128)}, /*index=5*/f32[1,192]{1,0:T(1,128)}) custom-call(f32[2,2,24,128]{3,2,1,0:T(8,128)} %get-tuple-element.17.gg, f32[2,24,128]{2,1,0:T(8,128)} %get-tuple-element.18.og, ...), custom_call_target="tpu_custom_call" | custom-call | tf_op jit(solution)/shard_map/unpack/pallas_call | solution.py:540

commit v4 on v3

--- a/solution.py
+++ b/solution.py
@@ -17,8 +17,8 @@
 STAT_Y, STAT_Z, SUM_Y, SUM_Z, PART, GATHER = 0, 1, 2, 3, 4, 5
 OUT_Y1, OUT_Z2, OUT_Z1, OUT_Y2 = 6, 7, 8, 9
 TAP_Z1, TAP_Y, TAP_Z2 = 10, 11, 12
-IN_Y, IN_Z, PROJ_Y, PROJ_Z, GLU_Z2, GLU_Y2 = 13, 14, 15, 16, 17, 18
-STAGES = 19
+IN_Y, IN_Z, IN_X, PROJ_Y, PROJ_Z, GLU_Z2, GLU_Y2 = 13, 14, 15, 16, 17, 18, 19
+STAGES = 20
 HALF = LANES // 2
 MESH = pl.DeviceIdType.MESH
 WIDE = (((1,), (1,)), ((), ()))
@@ -26,12 +26,13 @@
 
 def body(
     nx, ny, nz, cnt_hbm, x_hbm, glu_hbm, taps_hbm, gain_hbm, shift_hbm, out_hbm, cot_hbm,
-    ig_ref, gg_ref, og_ref, kg_ref, gb_ref,
+    ig_hbm, gg_hbm, og_hbm, kg_hbm, gb_hbm,
+    gg_ref, og_ref, gb_ref,
     cnt, xs, glus, taps, gains, shifts, outs, cots,
     par, xt, glut, up, hs, gpad, gcpad, convs, normeds, dacts, acts, gas, gss, gps,
     st_y, st_z, su_y, su_z, rx, share,
-    xw, xy, xz, xl, gp, py, pz, prod, gz1, gz2, gy1, gy2,
-    osend, oy1, oy1s, oz2, oz1, oz1s, oy2, ks, kz, ky, kg, local_sem, send_sem, recv_sem,
+    xw, xp, xg, xl, gp, py, pz, prod, gz1, gz2, gy1, gy2,
+    osend, otail, oy1, oy1s, oz2, oz1, oz1s, oy2, ks, kz, ky, kg, local_sem, send_sem, recv_sem,
 ):
     dp = lax.axis_index("dp")
     core = lax.axis_index("pipe")
@@ -97,6 +98,12 @@
     ]
     for load in loads:
         load.start()
+
+    results = []
+
+    def done(i, src, dst):
+        results.append(pltpu.make_async_copy(src, dst, local_sem.at[8 + i]))
+        results[-1].start()
 
     barrier = pltpu.get_barrier_semaphore()
     for axis in ("x", "y", "z"):
@@ -164,36 +171,39 @@
             at = pl.multiple_of(c * LANES, LANES)
             dst[pl.ds(at, LANES), :] = jnp.transpose(src[:, pl.ds(at, LANES)])
 
-    def send_inputs():
-        flip(xs, xt)
-
-        @pl.loop(0, nz)
-        def _(z):
-            part = xt[pl.ds(pl.multiple_of(z * slab, slab), slab), :].astype(jnp.float32)
-            xw[z] = part.reshape(ny, rows, LANES).astype(jnp.bfloat16)
-
-        start_y()
-        start_z()
-
-    def slab_of(i):
-        return pl.ds(pl.multiple_of(i * slab, slab), slab)
-
-    start_y = push(IN_Y, "y", lambda i: xw.at[:, i], slot(xy), False)
-    start_z = push(IN_Z, "z", lambda i: xt.at[slab_of(i)], slot(xz), False)
+    flip(xs, xt)
+
+    @pl.loop(0, nz)
+    def _(z):
+        part = xt[pl.ds(pl.multiple_of(z * slab, slab), slab), :].astype(jnp.float32)
+        xw[z] = part.reshape(ny, rows, LANES).astype(jnp.bfloat16)
+
+    xp[0, my] = xw[mx, my]
+    xp[1, mz] = xw[mz, mx]
+    in_y = push(IN_Y, "y", lambda i: xw.at[mx, i], lambda i: xp.at[0, i], False)
+    in_z = push(IN_Z, "z", lambda i: xw.at[i, mx], lambda i: xp.at[1, i], False)
+    in_x = push(IN_X, "x", lambda i: xp, slot(xg), False)
+
+    def share_inputs():
+        take(IN_Y, "y", lambda i: xp.at[0, i])
+        take(IN_Z, "z", lambda i: xp.at[1, i])
+        in_x()
 
     def place_inputs():
-        take(IN_Y, "y", slot(xy))
-        take(IN_Z, "z", slot(xz))
-        xy[my] = xw[:, my]
-        xz[mz] = xt[slab_of(mz), :]
-        for i in range(ny):
-            part = xy[i].astype(jnp.float32).reshape(nz * rows, LANES)
-            xl[0, 0 : nz * rows, i * LANES : (i + 1) * LANES] = part.astype(jnp.bfloat16)
-        for i in range(nz):
-            xl[1, :, i * LANES : (i + 1) * LANES] = xz[i]
+        take(IN_X, "x", slot(xg))
+        xg[mx] = xp[...]
+        for h in range(2):
+            for i in range(ny):
+                part = xg[:, h, i].astype(jnp.float32).reshape(nx * rows, LANES)
+                xl[h, :, i * LANES : (i + 1) * LANES] = part.astype(jnp.bfloat16)
 
     pl.semaphore_wait(barrier, (nx - 1) + (ny - 1) + (nz - 1) + nx)
     push(STAT_Y, "y", lambda i: st_y.at[my], slot(st_y))
+
+    @pl.when(core == 0)
+    def _():
+        in_y()
+        in_z()
 
     for load in loads[6:]:
         load.wait()
@@ -216,6 +226,10 @@
         glut[pl.ds(at, LANES), 2 * LANES :] = jnp.transpose(
             jnp.concatenate([glus[0, LANES:, pl.ds(at, LANES)], glus[1, LANES:, pl.ds(at, LANES)]], axis=0)
         )
+
+    @pl.when(core == 0)
+    def _():
+        share_inputs()
 
     take(STAT_Z, "z", slot(st_z))
     stats = summed(st_z, nz)
@@ -246,7 +260,6 @@
 
     @pl.when(core == 0)
     def _():
-        send_inputs()
         place_inputs()
         ga = jnp.zeros((channels, FRAMES), jnp.float32)
         for i in range(0, nx, 2):
@@ -281,19 +294,30 @@
     def _(z):
         at = pl.ds(pl.multiple_of(z * slab, slab), slab)
         part = jnp.dot(up[at, :], acts[...], preferred_element_type=jnp.float32)
-        for i in range(2):
-            osend[i, z] = part[:, i * LANES : (i + 1) * LANES].reshape(ny, rows, LANES).astype(jnp.bfloat16)
-
-    push(OUT_Y1, "y", lambda i: osend.at[0, :, i], slot(oy1))
-    push(OUT_Z1, "z", lambda i: osend.at[1, i], slot(oz1))
+        osend[z] = part[:, 0:LANES].reshape(ny, rows, LANES).astype(jnp.bfloat16)
+        tail = part[0 : slab // 2, LANES:] + pltpu.roll(part[slab // 2 :, LANES:], HALF, 1)
+        otail[z] = tail.reshape(ny // 2, rows, LANES).astype(jnp.bfloat16)
+
+    out_y = push(OUT_Y1, "y", lambda i: osend.at[:, i], slot(oy1), False)
+    out_z = push(OUT_Z1, "z", slot(otail), slot(oz1), False)
+
+    @pl.when(core == 0)
+    def _():
+        out_y()
+        out_z()
+
+    take(SUM_Z, "z", slot(su_z))
 
     @pl.when(core == 1)
     def _():
-        send_inputs()
-
-    take(SUM_Z, "z", slot(su_z))
+        out_y()
+        out_z()
+        in_y()
+        in_z()
+
     sums = summed(su_z, nz)
     gb_ref[...] = sums
+    done(4, gb_ref, gb_hbm)
     for j in range(2):
         gcpad[j, PAD : PAD + FRAMES, :] = (
             factors[j]
@@ -358,7 +382,7 @@
             acc = acc + rx[0, s].astype(jnp.float32)
         final = (up[block(mx), :].astype(jnp.float32) + acc).astype(jnp.bfloat16)
         share[...] = final
-        ig_ref[...] = final
+        pltpu.make_async_copy(share, ig_hbm, local_sem.at[8]).start()
 
     @pl.when(core == 1)
     def _():
@@ -368,7 +392,7 @@
         def _(i):
             gather_copy(i).start()
 
-        place_inputs()
+        share_inputs()
 
     for j in range(2):
         gc = gcpad[j, PAD : PAD + FRAMES, :]
@@ -390,18 +414,20 @@
             acc = acc + buf[lax.rem(me + r, n)].astype(jnp.float32)
         return acc
 
-    oy1s[...] = reduced(OUT_Y1, "y", oy1, osend[0, :, my]).astype(jnp.bfloat16)
+    early = list(pending)
+    del pending[:]
+    oy1s[...] = reduced(OUT_Y1, "y", oy1, osend[:, my]).astype(jnp.bfloat16)
     push(OUT_Z2, "z", slot(oy1s), slot(oz2))
-    oz1s[...] = reduced(OUT_Z1, "z", oz1, osend[1, mz]).astype(jnp.bfloat16)
-    push(OUT_Y2, "y", slot(oz1s), slot(oy2))
-
-    @pl.when(core == 0)
-    def _():
-        input_grad()
-
+    oz1s[...] = reduced(OUT_Z1, "z", oz1, otail[mz]).astype(jnp.bfloat16)
+    push(OUT_Y2, "y", lambda i: oz1s.at[lax.rem(i, ny // 2)], slot(oy2))
     take(TAP_Z1, "z", slot(kz))
     ky[my] = summed(kz, nz)
     push(TAP_Y, "y", lambda i: ky.at[my], slot(ky))
+
+    @pl.when(core == 1)
+    def _():
+        place_inputs()
+
 
     low = lax.broadcasted_iota(jnp.int32, (FRAMES // 2, LANES), 1) < HALF
 
@@ -425,19 +451,32 @@
     push(GLU_Y2, "y", slot(gz1), slot(gy2))
     products(0, PROJ_Y, "y", py, gy1)
     push(GLU_Z2, "z", slot(gy1), slot(gz2))
+
+    @pl.when(core == 0)
+    def _():
+        input_grad()
+
     take(TAP_Y, "y", slot(ky))
     kg[mz] = summed(ky, ny)
     push(TAP_Z2, "z", lambda i: kg.at[mz], slot(kg))
 
+    for wait in early:
+        wait()
     og_ref[0] = reduced(OUT_Z2, "z", oz2, oy1s[mz])
-    og_ref[1] = reduced(OUT_Y2, "y", oy2, oz1s[my])
+    tail = reduced(OUT_Y2, "y", oy2, oz1s[lax.rem(my, ny // 2)])
+    og_ref[1] = jnp.where(my < ny // 2, tail, pltpu.roll(tail, HALF, 1))
+    done(2, og_ref, og_hbm)
     gg_ref[1] = reduced(GLU_Y2, "y", gy2, gz1[my])
     gg_ref[0] = reduced(GLU_Z2, "z", gz2, gy1[mz])
+    done(1, gg_ref, gg_hbm)
     take(TAP_Z2, "z", slot(kg))
-    kg_ref[...] = kg[...]
+    done(3, kg, kg_hbm)
 
     for wait in pending:
         wait()
+    for result in results:
+        result.wait()
+    pltpu.make_async_copy(share, ig_hbm, local_sem.at[8]).wait()
 
     @pl.when(core == 1)
     def _():
@@ -470,6 +509,7 @@
     depth = saved_inputs.shape[-1]
     channels = depth // nx
     rows = depth // (ny * nz)
+    assert nx == ny == nz
 
     f32, bf16 = jnp.float32, jnp.bfloat16
     operands = (
@@ -500,8 +540,11 @@
             jax.ShapeDtypeStruct((8, LANES), f32),
         ),
         in_specs=[pl.BlockSpec(memory_space=pl.ANY)] * len(operands),
-        out_specs=(vmem,) * 5,
+        out_specs=(pl.BlockSpec(memory_space=pl.ANY),) * 5,
         scratch_shapes=[
+            pltpu.VMEM((2, 2, rows, LANES), f32),
+            pltpu.VMEM((2, rows, LANES), f32),
+            pltpu.VMEM((8, LANES), f32),
             pltpu.SMEM((1,), jnp.int32),
             *(pltpu.VMEM(a.shape, a.dtype) for a in operands[1:]),
             pltpu.VMEM((2, KERNEL + 8, LANES), f32),
@@ -517,21 +560,21 @@
             *(pltpu.VMEM((n, 8, LANES), f32) for n in (ny, nz, ny, nz)),
             pltpu.VMEM((2, nx, channels, FRAMES), bf16),
             pltpu.VMEM((channels, FRAMES), bf16),
-            wire(nz, ny), wire(ny, nz),
-            pltpu.VMEM((nz, ny * rows, LANES), bf16),
-            pltpu.VMEM((2, max(ny, nz) * rows, max(ny, nz) * LANES), bf16),
+            wire(nz, ny), wire(2, ny), wire(nx, 2, ny),
+            pltpu.VMEM((2, nx * rows, ny * LANES), bf16),
             pltpu.VMEM((2, FRAMES + FRAMES // 2, LANES), bf16),
             pltpu.VMEM((ny, FRAMES + FRAMES // 2, LANES), bf16),
             pltpu.VMEM((nz, FRAMES + FRAMES // 2, LANES), bf16),
             pltpu.VMEM((2, max(ny, nz) * FRAMES, 2 * LANES), bf16),
             wire(ny, 2), wire(nz, 2), wire(nz, 2), wire(ny, 2),
-            wire(2, nz, ny),
-            wire(ny, nz), wire(nz), wire(nz), wire(nz, ny), wire(ny), wire(ny),
+            wire(nz, ny), wire(nz, ny // 2),
+            wire(ny, nz), wire(nz), wire(nz),
+            wire(nz, ny // 2), wire(ny // 2), wire(ny),
             pltpu.VMEM((nz, 2, KERNEL // nz, LANES), f32),
             pltpu.VMEM((nz, 2, KERNEL // nz, LANES), f32),
             pltpu.VMEM((ny, 2, KERNEL // nz, LANES), f32),
             pltpu.VMEM((nz, 2, KERNEL // nz, LANES), f32),
-            pltpu.SemaphoreType.DMA((len(operands),)),
+            pltpu.SemaphoreType.DMA((len(operands) + 5,)),
             sem, sem,
         ],
         compiler_params=pltpu.CompilerParams(collective_id=0, has_side_effects=True),

time: 89.2 us -> 89.3 us (level); the launches traced: 89 us -> 88 us
  Pallas kernels: 87.7 us -> 86.7 us
    pallas_call x1, Pallas kernels: 86.2 us -> 85.1 us  [shards(): pl.pallas_call(functools.partial(body, nx, ny, nz), out_shape=(jax.ShapeD...]
where the time goes in v4:
time: 89.3 us; the launch traced here: 88 us
  Pallas kernels  86.7 us (97%)
  between operations  1.29 us (1%)
    pallas_call x1, Pallas kernels, shards(): pl.pallas_call(functools.partial(body, nx, ny, nz), out_shape=(jax.ShapeD...  85.1 us

profile of v4, /device:TPU:14, one launch (start us, length us, event | category | flops | bytes accessed | tf_op | source)
XLA Modules:
  0.0 88.0 jit_solution(6310368185651477961)
XLA Ops:
  1.3 85.1 %conformer_backward.1 = (bf16[192,128]{1,0:T(8,128)(2,1)}, f32[2,2,24,128]{3,2,1,0:T(8,128)}, f32[2,24,128]{2,1,0:T(8,128)}, f32[8,2,4,128]{3,2,1,0:T(4,128)}, f32[8,128]{1,0:T(8,128)}) custom-call(s32[1]{0:T(128)S(6)} %copy.14.cnt_hbm, bf16[128,1536]{1,0:T(8,128)(2,1)} %bitcast.17, bf16[2,192,1536]{2,1,0:T(8,128)(2,1)} %bitcast.15, f32[32,192]{1,0:T(8,128)} %bitcast.19, ...), custom_call_target="tpu_custom_call" | custom-call | tf_op jit(solution)/shard_map/conformer_backward/pallas_call | solution.py:533
  86.4 1.5 %unpack.1 = (bf16[192,128]{1,0:T(8,128)(2,1)}, f32[24,2,192]{2,1,0:T(2,128)}, f32[24,192]{1,0:T(8,128)}, f32[32,192]{1,0:T(8,128)}, f32[1,192]{1,0:T(1,128)}, /*index=5*/f32[1,192]{1,0:T(1,128)}) custom-call(f32[2,2,24,128]{3,2,1,0:T(8,128)} %get-tuple-element.17.gg, f32[2,24,128]{2,1,0:T(8,128)} %get-tuple-element.18.og, ...), custom_call_target="tpu_custom_call" | custom-call | tf_op jit(solution)/shard_map/unpack/pallas_call | solution.py:583

commit v5 on v4

--- a/solution.py
+++ b/solution.py
@@ -31,8 +31,8 @@
     cnt, xs, glus, taps, gains, shifts, outs, cots,
     par, xt, glut, up, hs, gpad, gcpad, convs, normeds, dacts, acts, gas, gss, gps,
     st_y, st_z, su_y, su_z, rx, share,
-    xw, xp, xg, xl, gp, py, pz, prod, gz1, gz2, gy1, gy2,
-    osend, otail, oy1, oy1s, oz2, oz1, oz1s, oy2, ks, kz, ky, kg, local_sem, send_sem, recv_sem,
+    xw, xp, xc, xg, xf, xl, gp, py, pz, prod, gz1, gz2, gy1, gy2,
+    osf, osend, otail, oy1, oy1s, oz2, oz1, oz1s, oy2, ks, kz, ky, kg, local_sem, send_sem, recv_sem,
 ):
     dp = lax.axis_index("dp")
     core = lax.axis_index("pipe")
@@ -176,25 +176,34 @@
     @pl.loop(0, nz)
     def _(z):
         part = xt[pl.ds(pl.multiple_of(z * slab, slab), slab), :].astype(jnp.float32)
-        xw[z] = part.reshape(ny, rows, LANES).astype(jnp.bfloat16)
-
+        xw[z, :, 0:rows, :] = part.reshape(ny, rows, LANES).astype(jnp.bfloat16)
+
+    if xw.shape[2] > rows:
+        xw[:, :, rows:, :] = jnp.zeros((nz, ny, xw.shape[2] - rows, LANES), jnp.bfloat16)
     xp[0, my] = xw[mx, my]
     xp[1, mz] = xw[mz, mx]
     in_y = push(IN_Y, "y", lambda i: xw.at[mx, i], lambda i: xp.at[0, i], False)
     in_z = push(IN_Z, "z", lambda i: xw.at[i, mx], lambda i: xp.at[1, i], False)
-    in_x = push(IN_X, "x", lambda i: xp, slot(xg), False)
+    in_x = push(IN_X, "x", lambda i: xc, slot(xg), False)
 
     def share_inputs():
         take(IN_Y, "y", lambda i: xp.at[0, i])
         take(IN_Z, "z", lambda i: xp.at[1, i])
+        xc[...] = xp[:, :, 0:rows, :].astype(jnp.float32).reshape(2 * slab, LANES).astype(jnp.bfloat16)
         in_x()
 
     def place_inputs():
         take(IN_X, "x", slot(xg))
-        xg[mx] = xp[...]
+        xg[mx] = xc[...]
+
+        @pl.loop(0, nx)
+        def _(i):
+            xf[i] = xg[i].astype(jnp.float32)
+
         for h in range(2):
             for i in range(ny):
-                part = xg[:, h, i].astype(jnp.float32).reshape(nx * rows, LANES)
+                at = h * slab + i * rows
+                part = xf[:, at : at + rows, :].reshape(nx * rows, LANES)
                 xl[h, :, i * LANES : (i + 1) * LANES] = part.astype(jnp.bfloat16)
 
     pl.semaphore_wait(barrier, (nx - 1) + (ny - 1) + (nz - 1) + nx)
@@ -232,6 +241,23 @@
         share_inputs()
 
     take(STAT_Z, "z", slot(st_z))
+    each = KERNEL // nz
+    span = 2 * each
+
+    def tap_sums(which, signals):
+        for j in range(2):
+            for b in range(8):
+                window = gpad[j, pl.ds(b, FRAMES + 24), :]
+                for a in range(KERNEL // 8):
+                    k = 8 * a + b
+                    ks[k // each, pl.ds(which * span + j * each + k % each, 1), :] = jnp.sum(
+                        signals[j] * window[8 * a : 8 * a + FRAMES], axis=0, keepdims=True
+                    )
+
+    def steady_tap_sums():
+        tap_sums(1, (valid, valid))
+        tap_sums(2, (valid * normeds[0], valid * normeds[1]))
+
     stats = summed(st_z, nz)
     total = stats[4:5]
     factors = []
@@ -260,6 +286,7 @@
 
     @pl.when(core == 0)
     def _():
+        steady_tap_sums()
         place_inputs()
         ga = jnp.zeros((channels, FRAMES), jnp.float32)
         for i in range(0, nx, 2):
@@ -286,26 +313,38 @@
     def _():
         flip(cots, up)
 
-    take(SUM_Y, "y", slot(su_y))
-    su_z[mz] = summed(su_y, ny)
-    push(SUM_Z, "z", lambda i: su_z.at[mz], slot(su_z))
+    tap_sums(0, (gss[0], gss[1]))
 
     @pl.loop(0, nz)
     def _(z):
         at = pl.ds(pl.multiple_of(z * slab, slab), slab)
         part = jnp.dot(up[at, :], acts[...], preferred_element_type=jnp.float32)
-        osend[z] = part[:, 0:LANES].reshape(ny, rows, LANES).astype(jnp.bfloat16)
+        osf[:, z] = part[:, 0:LANES].reshape(ny, rows, LANES)
         tail = part[0 : slab // 2, LANES:] + pltpu.roll(part[slab // 2 :, LANES:], HALF, 1)
-        otail[z] = tail.reshape(ny // 2, rows, LANES).astype(jnp.bfloat16)
-
-    out_y = push(OUT_Y1, "y", lambda i: osend.at[:, i], slot(oy1), False)
+        otail[z] = tail.astype(jnp.bfloat16)
+
+    @pl.loop(0, ny)
+    def _(i):
+        osend[i] = osf[i].reshape(nz * rows, LANES).astype(jnp.bfloat16)
+
+    out_y = push(OUT_Y1, "y", slot(osend), slot(oy1), False)
     out_z = push(OUT_Z1, "z", slot(otail), slot(oz1), False)
+
+    take(SUM_Y, "y", slot(su_y))
+    su_z[mz] = summed(su_y, ny)
+    push(SUM_Z, "z", lambda i: su_z.at[mz], slot(su_z))
 
     @pl.when(core == 0)
     def _():
         out_y()
         out_z()
 
+    @pl.when(core == 1)
+    def _():
+        steady_tap_sums()
+
+    kz[mz] = ks[mz]
+    push(TAP_Z1, "z", slot(ks), slot(kz))
     take(SUM_Z, "z", slot(su_z))
 
     @pl.when(core == 1)
@@ -353,21 +392,24 @@
         proj_y()
         proj_z()
 
-    def partial_of(i):
-        return lax.dot_general(
-            glut[block(i), :], gps[...], WIDE, preferred_element_type=jnp.float32
-        ).astype(jnp.bfloat16)
-
     def part_copy(i):
         return copy(PART, "x", i, lambda p: rx.at[1, p], lambda p: rx.at[0, p])
 
-    def send_part(i):
-        rx[1, i] = partial_of(i)
-        part_copy(i).start()
-
-    around("x", send_part)
+    pairs = nx // 2
+    for off in sorted(range(pairs), key=lambda k: min(k, pairs - k), reverse=True):
+        i = 2 * lax.rem(lax.div(mx, 2) + off, pairs)
+        at = pl.ds(pl.multiple_of(i * channels, 2 * channels), 2 * channels)
+        part = lax.dot_general(
+            glut[at, :], gps[...], WIDE, preferred_element_type=jnp.float32
+        ).astype(jnp.bfloat16)
+        for k in range(2):
+            rx[1, i + k] = part[k * channels : (k + 1) * channels]
+            if off:
+                part_copy(i + k).start()
+            else:
+                pl.when(i + k != mx)(lambda k=k: part_copy(i + k).start())
     pending.append(lambda: around("x", lambda i: part_copy(i).wait_send()))
-    rx[0, mx] = partial_of(mx)
+    rx[0, mx] = rx[1, mx]
 
     @pl.when(core == 1)
     def _():
@@ -394,18 +436,6 @@
 
         share_inputs()
 
-    for j in range(2):
-        gc = gcpad[j, PAD : PAD + FRAMES, :]
-        for b in range(8):
-            window = gpad[j, pl.ds(b, FRAMES + 24), :]
-            for a in range(KERNEL // 8):
-                k, each = 8 * a + b, KERNEL // nz
-                ks[k // each, j, pl.ds(k % each, 1), :] = jnp.sum(
-                    gc * window[8 * a : 8 * a + FRAMES], axis=0, keepdims=True
-                )
-    push(TAP_Z1, "z", slot(ks), slot(kz))
-    kz[mz] = ks[mz]
-
     def reduced(stage, axis, buf, own):
         take(stage, axis, slot(buf))
         me, n, _ = axes[axis]
@@ -416,13 +446,13 @@
 
     early = list(pending)
     del pending[:]
-    oy1s[...] = reduced(OUT_Y1, "y", oy1, osend[:, my]).astype(jnp.bfloat16)
-    push(OUT_Z2, "z", slot(oy1s), slot(oz2))
-    oz1s[...] = reduced(OUT_Z1, "z", oz1, otail[mz]).astype(jnp.bfloat16)
-    push(OUT_Y2, "y", lambda i: oz1s.at[lax.rem(i, ny // 2)], slot(oy2))
     take(TAP_Z1, "z", slot(kz))
     ky[my] = summed(kz, nz)
     push(TAP_Y, "y", lambda i: ky.at[my], slot(ky))
+    oy1s[...] = reduced(OUT_Y1, "y", oy1, osend[my]).reshape(nz, rows, LANES)
+    push(OUT_Z2, "z", slot(oy1s), slot(oz2))
+    oz1s[...] = reduced(OUT_Z1, "z", oz1, otail[mz]).reshape(ny // 2, rows, LANES)
+    push(OUT_Y2, "y", lambda i: oz1s.at[lax.rem(i, ny // 2)], slot(oy2))
 
     @pl.when(core == 1)
     def _():
@@ -444,24 +474,35 @@
                 low, pltpu.roll(tail, HALF, 1), 0.0
             ).astype(jnp.bfloat16)
         total = jnp.dot(xl[i, :, 0 : n * FRAMES], prod[i, 0 : n * FRAMES], preferred_element_type=jnp.float32)
-        for k in range(2):
-            out[:, k] = total[:, k * LANES : (k + 1) * LANES].reshape(-1, rows, LANES).astype(jnp.bfloat16)
-
+        parts = [total[:, k * LANES : (k + 1) * LANES].reshape(-1, rows, LANES) for k in range(2)]
+        out[...] = jnp.concatenate(parts, axis=1).astype(jnp.bfloat16)
+
+    for wait in early:
+        wait()
     products(1, PROJ_Z, "z", pz, gz1)
     push(GLU_Y2, "y", slot(gz1), slot(gy2))
     products(0, PROJ_Y, "y", py, gy1)
     push(GLU_Z2, "z", slot(gy1), slot(gz2))
 
+    take(TAP_Y, "y", slot(ky))
+    tap_total = summed(ky, ny)
+    upper = lax.broadcasted_iota(jnp.int32, (span, LANES), 0) < each
+
+    def per_tile(first, second):
+        return jnp.where(upper, first, second)
+
+    kg[mz] = per_tile(*factors) * (
+        tap_total[0:span]
+        - per_tile(sums[0:1] / total, sums[1:2] / total) * tap_total[span : 2 * span]
+        - per_tile(sums[2:3] / total, sums[3:4] / total) * tap_total[2 * span :]
+    )
+    push(TAP_Z2, "z", lambda i: kg.at[mz], slot(kg))
+
     @pl.when(core == 0)
     def _():
         input_grad()
 
-    take(TAP_Y, "y", slot(ky))
-    kg[mz] = summed(ky, ny)
-    push(TAP_Z2, "z", lambda i: kg.at[mz], slot(kg))
-
-    for wait in early:
-        wait()
+
     og_ref[0] = reduced(OUT_Z2, "z", oz2, oy1s[mz])
     tail = reduced(OUT_Y2, "y", oy2, oz1s[lax.rem(my, ny // 2)])
     og_ref[1] = jnp.where(my < ny // 2, tail, pltpu.roll(tail, HALF, 1))
@@ -488,14 +529,16 @@
 def unpack(gg, og, kg, gb, ig, ig_out, glu_out, out_out, taps_out, gain_out, bias_out):
     ig_out[...] = ig[...]
     for i in range(2):
-        glu_out[:, i, 0:LANES] = gg[i, 0]
-        glu_out[:, i, LANES:] = gg[i, 1, :, 0:HALF]
+        rows = gg.shape[1] // 2
+        glu_out[:, i, 0:LANES] = gg[i, 0:rows]
+        glu_out[:, i, LANES:] = gg[i, rows:, 0:HALF]
     out_out[:, 0:LANES] = og[0]
     out_out[:, LANES:] = og[1, :, 0:HALF]
     for i in range(kg.shape[0]):
-        at = pl.ds(i * kg.shape[2], kg.shape[2])
-        taps_out[at, 0:LANES] = kg[i, 0]
-        taps_out[at, LANES:] = kg[i, 1, :, 0:HALF]
+        each = kg.shape[1] // 2
+        at = pl.ds(i * each, each)
+        taps_out[at, 0:LANES] = kg[i, 0:each]
+        taps_out[at, LANES:] = kg[i, each:, 0:HALF]
     for ref, at in ((bias_out, 0), (gain_out, 2)):
         ref[:, 0:LANES] = gb[at : at + 1, :]
         ref[:, LANES:] = gb[at + 1 : at + 2, 0:HALF]
@@ -509,6 +552,7 @@
     depth = saved_inputs.shape[-1]
     channels = depth // nx
     rows = depth // (ny * nz)
+    whole = -(-rows // 16) * 16
     assert nx == ny == nz
 
     f32, bf16 = jnp.float32, jnp.bfloat16
@@ -526,23 +570,20 @@
     big = pltpu.VMEM((2, FRAMES, LANES), f32)
     padded = pltpu.VMEM((2, FRAMES + 2 * PAD, LANES), f32)
 
-    def wire(*shape):
-        return pltpu.VMEM(shape + (rows, LANES), bf16)
-
     sem = pltpu.SemaphoreType.DMA((STAGES, max(nx, ny, nz)))
     ig, gg, og, kg, gb = pl.pallas_call(
         functools.partial(body, nx, ny, nz),
         out_shape=(
             jax.ShapeDtypeStruct((channels, FRAMES), bf16),
-            jax.ShapeDtypeStruct((2, 2, rows, LANES), f32),
+            jax.ShapeDtypeStruct((2, 2 * rows, LANES), f32),
             jax.ShapeDtypeStruct((2, rows, LANES), f32),
-            jax.ShapeDtypeStruct((nz, 2, KERNEL // nz, LANES), f32),
+            jax.ShapeDtypeStruct((nz, 2 * KERNEL // nz, LANES), f32),
             jax.ShapeDtypeStruct((8, LANES), f32),
         ),
         in_specs=[pl.BlockSpec(memory_space=pl.ANY)] * len(operands),
         out_specs=(pl.BlockSpec(memory_space=pl.ANY),) * 5,
         scratch_shapes=[
-            pltpu.VMEM((2, 2, rows, LANES), f32),
+            pltpu.VMEM((2, 2 * rows, LANES), f32),
             pltpu.VMEM((2, rows, LANES), f32),
             pltpu.VMEM((8, LANES), f32),
             pltpu.SMEM((1,), jnp.int32),
@@ -560,20 +601,27 @@
             *(pltpu.VMEM((n, 8, LANES), f32) for n in (ny, nz, ny, nz)),
             pltpu.VMEM((2, nx, channels, FRAMES), bf16),
             pltpu.VMEM((channels, FRAMES), bf16),
-            wire(nz, ny), wire(2, ny), wire(nx, 2, ny),
+            *(pltpu.VMEM(n + (whole, LANES), bf16) for n in ((nz, ny), (2, ny))),
+            pltpu.VMEM((2 * ny * rows, LANES), bf16),
+            pltpu.VMEM((nx, 2 * ny * rows, LANES), bf16),
+            pltpu.VMEM((nx, 2 * ny * rows, LANES), f32),
             pltpu.VMEM((2, nx * rows, ny * LANES), bf16),
             pltpu.VMEM((2, FRAMES + FRAMES // 2, LANES), bf16),
             pltpu.VMEM((ny, FRAMES + FRAMES // 2, LANES), bf16),
             pltpu.VMEM((nz, FRAMES + FRAMES // 2, LANES), bf16),
             pltpu.VMEM((2, max(ny, nz) * FRAMES, 2 * LANES), bf16),
-            wire(ny, 2), wire(nz, 2), wire(nz, 2), wire(ny, 2),
-            wire(nz, ny), wire(nz, ny // 2),
-            wire(ny, nz), wire(nz), wire(nz),
-            wire(nz, ny // 2), wire(ny // 2), wire(ny),
-            pltpu.VMEM((nz, 2, KERNEL // nz, LANES), f32),
-            pltpu.VMEM((nz, 2, KERNEL // nz, LANES), f32),
-            pltpu.VMEM((ny, 2, KERNEL // nz, LANES), f32),
-            pltpu.VMEM((nz, 2, KERNEL // nz, LANES), f32),
+            *(pltpu.VMEM((n, 2 * rows, LANES), bf16) for n in (ny, nz, nz, ny)),
+            pltpu.VMEM((ny, nz, rows, LANES), f32),
+            pltpu.VMEM((ny, nz * rows, LANES), bf16),
+            pltpu.VMEM((nz, ny * rows // 2, LANES), bf16),
+            pltpu.VMEM((ny, nz * rows, LANES), bf16),
+            pltpu.VMEM((nz, rows, LANES), f32),
+            pltpu.VMEM((nz, rows, LANES), f32),
+            pltpu.VMEM((nz, ny * rows // 2, LANES), bf16),
+            pltpu.VMEM((ny // 2, rows, LANES), f32),
+            pltpu.VMEM((ny, rows, LANES), f32),
+            *(pltpu.VMEM((n, 6 * KERNEL // nz, LANES), f32) for n in (nz, nz, ny)),
+            pltpu.VMEM((nz, 2 * KERNEL // nz, LANES), f32),
             pltpu.SemaphoreType.DMA((len(operands) + 5,)),
             sem, sem,
         ],

time: 89.3 us -> 86.3 us (0.966)
  the two profiles are of different devices: /device:TPU:14 before, /device:TPU:8 now
where the time goes in v5:
time: 86.3 us; the launch traced here: 86 us
  Pallas kernels  84.7 us (98%)
  between operations  1.29 us (1%)
    pallas_call x1, Pallas kernels, shards(): pl.pallas_call(functools.partial(body, nx, ny, nz), out_shape=(jax.ShapeD...  83.2 us

profile of v5, /device:TPU:8, one launch (start us, length us, event | category | flops | bytes accessed | tf_op | source)
XLA Modules:
  0.0 86.0 jit_solution(2184406220725096288)
XLA Ops:
  1.3 83.2 %conformer_backward.1 = (bf16[192,128]{1,0:T(8,128)(2,1)}, f32[2,48,128]{2,1,0:T(8,128)}, f32[2,24,128]{2,1,0:T(8,128)}, f32[8,8,128]{2,1,0:T(8,128)}, f32[8,128]{1,0:T(8,128)}) custom-call(s32[1]{0:T(128)S(6)} %copy.14.cnt_hbm, bf16[128,1536]{1,0:T(8,128)(2,1)} %bitcast.17, bf16[2,192,1536]{2,1,0:T(8,128)(2,1)} %bitcast.15, f32[32,192]{1,0:T(8,128)} %bitcast.19, ...), custom_call_target="tpu_custom_call" | custom-call | tf_op jit(solution)/shard_map/conformer_backward/pallas_call | solution.py:574
  84.5 1.5 %unpack.1 = (bf16[192,128]{1,0:T(8,128)(2,1)}, f32[24,2,192]{2,1,0:T(2,128)}, f32[24,192]{1,0:T(8,128)}, f32[32,192]{1,0:T(8,128)}, f32[1,192]{1,0:T(1,128)}, /*index=5*/f32[1,192]{1,0:T(1,128)}) custom-call(f32[2,48,128]{2,1,0:T(8,128)} %get-tuple-element.17.gg, f32[2,24,128]{2,1,0:T(8,128)} %get-tuple-element.18.og, f32[8,8,128]{2,1,0:T(8,128)} %get-tuple-element.19.kg, ...), custom_call_target="tpu_custom_call" | custom-call | tf_op jit(solution)/shard_map/unpack/pallas_call | solution.py:631

commit v6 on v5

--- a/solution.py
+++ b/solution.py
@@ -64,30 +64,35 @@
             off = lax.div(i, 2)
             step(lax.rem(me + n // 2 + jnp.where(lax.rem(i, 2) == 0, off, n - off), n))
 
-    def copy(stage, axis, peer, src, dst):
+    def copy(stage, axis, peer, src, buf):
         me, _, where = axes[axis]
         return pltpu.make_async_remote_copy(
-            src_ref=src(peer), dst_ref=dst(me),
-            send_sem=send_sem.at[stage, peer], recv_sem=recv_sem.at[stage, me],
+            src_ref=src(peer), dst_ref=buf.at[me],
+            send_sem=send_sem.at[stage], recv_sem=recv_sem.at[stage],
             device_id=where(peer), device_id_type=MESH,
         )
 
-    def push(stage, axis, src, dst, now=True):
+    def every(stage, refs, target):
+        return pltpu.make_async_remote_copy(
+            src_ref=refs, dst_ref=refs, send_sem=send_sem.at[stage], recv_sem=recv_sem.at[stage],
+            device_id=target, device_id_type=MESH,
+        )
+
+    def all_of(stage, axis, buf):
+        me, n, where = axes[axis]
+        return every(stage, buf.at[pl.ds(0, n - 1)], where(lax.rem(me + 1, n)))
+
+    def push(stage, axis, src, buf, now=True):
         def start():
-            around(axis, lambda p: copy(stage, axis, p, src, dst).start())
-
-        pending.append(lambda: around(axis, lambda p: copy(stage, axis, p, src, dst).wait_send()))
+            around(axis, lambda p: copy(stage, axis, p, src, buf).start())
+
+        pending.append(lambda: all_of(stage, axis, buf).wait_send())
         if now:
             start()
         return start
 
-    def take(stage, axis, dst):
-        where = axes[axis][2]
-        around(axis, lambda p: pltpu.make_async_remote_copy(
-            src_ref=dst(p), dst_ref=dst(p),
-            send_sem=send_sem.at[stage, p], recv_sem=recv_sem.at[stage, p],
-            device_id=where(p), device_id_type=MESH,
-        ).wait_recv())
+    def take(stage, axis, buf):
+        all_of(stage, axis, buf).wait_recv()
 
     loads = [
         pltpu.make_async_copy(a, b, local_sem.at[i])
@@ -182,18 +187,18 @@
         xw[:, :, rows:, :] = jnp.zeros((nz, ny, xw.shape[2] - rows, LANES), jnp.bfloat16)
     xp[0, my] = xw[mx, my]
     xp[1, mz] = xw[mz, mx]
-    in_y = push(IN_Y, "y", lambda i: xw.at[mx, i], lambda i: xp.at[0, i], False)
-    in_z = push(IN_Z, "z", lambda i: xw.at[i, mx], lambda i: xp.at[1, i], False)
-    in_x = push(IN_X, "x", lambda i: xc, slot(xg), False)
+    in_y = push(IN_Y, "y", lambda i: xw.at[mx, i], xp.at[0], False)
+    in_z = push(IN_Z, "z", lambda i: xw.at[i, mx], xp.at[1], False)
+    in_x = push(IN_X, "x", lambda i: xc, xg, False)
 
     def share_inputs():
-        take(IN_Y, "y", lambda i: xp.at[0, i])
-        take(IN_Z, "z", lambda i: xp.at[1, i])
+        take(IN_Y, "y", xp.at[0])
+        take(IN_Z, "z", xp.at[1])
         xc[...] = xp[:, :, 0:rows, :].astype(jnp.float32).reshape(2 * slab, LANES).astype(jnp.bfloat16)
         in_x()
 
     def place_inputs():
-        take(IN_X, "x", slot(xg))
+        take(IN_X, "x", xg)
         xg[mx] = xc[...]
 
         @pl.loop(0, nx)
@@ -207,7 +212,7 @@
                 xl[h, :, i * LANES : (i + 1) * LANES] = part.astype(jnp.bfloat16)
 
     pl.semaphore_wait(barrier, (nx - 1) + (ny - 1) + (nz - 1) + nx)
-    push(STAT_Y, "y", lambda i: st_y.at[my], slot(st_y))
+    push(STAT_Y, "y", lambda i: st_y.at[my], st_y)
 
     @pl.when(core == 0)
     def _():
@@ -223,9 +228,9 @@
         gas[0] = ga[:, 0:LANES]
         gas[1, :, 0:HALF] = ga[:, LANES:]
 
-    take(STAT_Y, "y", slot(st_y))
+    take(STAT_Y, "y", st_y)
     st_z[mz] = summed(st_y, ny)
-    push(STAT_Z, "z", lambda i: st_z.at[mz], slot(st_z))
+    push(STAT_Z, "z", lambda i: st_z.at[mz], st_z)
 
     @pl.loop(0, depth // LANES)
     def _(c):
@@ -240,7 +245,7 @@
     def _():
         share_inputs()
 
-    take(STAT_Z, "z", slot(st_z))
+    take(STAT_Z, "z", st_z)
     each = KERNEL // nz
     span = 2 * each
 
@@ -280,7 +285,7 @@
     def gather_copy(i):
         return pltpu.make_async_remote_copy(
             src_ref=share, dst_ref=up.at[block(mx)],
-            send_sem=send_sem.at[GATHER, i], recv_sem=recv_sem.at[GATHER, mx],
+            send_sem=send_sem.at[GATHER], recv_sem=recv_sem.at[GATHER],
             device_id=(dp, 0, i), device_id_type=MESH,
         )
 
@@ -288,16 +293,8 @@
     def _():
         steady_tap_sums()
         place_inputs()
-        ga = jnp.zeros((channels, FRAMES), jnp.float32)
-        for i in range(0, nx, 2):
-            for k in (i, i + 1):
-                pltpu.make_async_remote_copy(
-                    src_ref=share, dst_ref=up.at[k * channels : (k + 1) * channels],
-                    send_sem=send_sem.at[GATHER, 0], recv_sem=recv_sem.at[GATHER, k],
-                    device_id=(dp, 1, k), device_id_type=MESH,
-                ).wait_recv()
-            pair = slice(i * channels, (i + 2) * channels)
-            ga = ga + jnp.dot(outs[:, pair], up[pair, :], preferred_element_type=jnp.float32)
+        every(GATHER, up, (dp, 1, mx)).wait_recv()
+        ga = jnp.dot(outs[...], up[...], preferred_element_type=jnp.float32)
         gas[0] = jnp.transpose(ga[0:LANES])
         gas[1, :, 0:HALF] = jnp.transpose(ga[LANES:])
 
@@ -307,7 +304,7 @@
         su_y[my, pl.ds(j, 1), :] = jnp.sum(gs, axis=0, keepdims=True)
         su_y[my, pl.ds(2 + j, 1), :] = jnp.sum(gs * normeds[j], axis=0, keepdims=True)
     su_y[my, pl.ds(4, 4), :] = jnp.zeros((4, LANES), jnp.float32)
-    push(SUM_Y, "y", lambda i: su_y.at[my], slot(su_y))
+    push(SUM_Y, "y", lambda i: su_y.at[my], su_y)
 
     @pl.when(core == 1)
     def _():
@@ -327,12 +324,12 @@
     def _(i):
         osend[i] = osf[i].reshape(nz * rows, LANES).astype(jnp.bfloat16)
 
-    out_y = push(OUT_Y1, "y", slot(osend), slot(oy1), False)
-    out_z = push(OUT_Z1, "z", slot(otail), slot(oz1), False)
-
-    take(SUM_Y, "y", slot(su_y))
+    out_y = push(OUT_Y1, "y", slot(osend), oy1, False)
+    out_z = push(OUT_Z1, "z", slot(otail), oz1, False)
+
+    take(SUM_Y, "y", su_y)
     su_z[mz] = summed(su_y, ny)
-    push(SUM_Z, "z", lambda i: su_z.at[mz], slot(su_z))
+    push(SUM_Z, "z", lambda i: su_z.at[mz], su_z)
 
     @pl.when(core == 0)
     def _():
@@ -344,8 +341,8 @@
         steady_tap_sums()
 
     kz[mz] = ks[mz]
-    push(TAP_Z1, "z", slot(ks), slot(kz))
-    take(SUM_Z, "z", slot(su_z))
+    push(TAP_Z1, "z", slot(ks), kz)
+    take(SUM_Z, "z", su_z)
 
     @pl.when(core == 1)
     def _():
@@ -384,8 +381,8 @@
         gp[i, FRAMES:, :] = (
             wide[1][0 : FRAMES // 2] + pltpu.roll(wide[1][FRAMES // 2 :], HALF, 1)
         ).astype(jnp.bfloat16)
-    proj_y = push(PROJ_Y, "y", lambda i: gp.at[0], slot(py), False)
-    proj_z = push(PROJ_Z, "z", lambda i: gp.at[1], slot(pz), False)
+    proj_y = push(PROJ_Y, "y", lambda i: gp.at[0], py, False)
+    proj_z = push(PROJ_Z, "z", lambda i: gp.at[1], pz, False)
 
     @pl.when(core == 0)
     def _():
@@ -393,7 +390,7 @@
         proj_z()
 
     def part_copy(i):
-        return copy(PART, "x", i, lambda p: rx.at[1, p], lambda p: rx.at[0, p])
+        return copy(PART, "x", i, lambda p: rx.at[1, p], rx.at[0])
 
     pairs = nx // 2
     for off in sorted(range(pairs), key=lambda k: min(k, pairs - k), reverse=True):
@@ -408,7 +405,7 @@
                 part_copy(i + k).start()
             else:
                 pl.when(i + k != mx)(lambda k=k: part_copy(i + k).start())
-    pending.append(lambda: around("x", lambda i: part_copy(i).wait_send()))
+    pending.append(lambda: all_of(PART, "x", rx.at[0]).wait_send())
     rx[0, mx] = rx[1, mx]
 
     @pl.when(core == 1)
@@ -418,7 +415,7 @@
 
 
     def input_grad():
-        take(PART, "x", lambda s: rx.at[0, s])
+        take(PART, "x", rx.at[0])
         acc = rx[0, 0].astype(jnp.float32)
         for s in range(1, nx):
             acc = acc + rx[0, s].astype(jnp.float32)
@@ -437,7 +434,7 @@
         share_inputs()
 
     def reduced(stage, axis, buf, own):
-        take(stage, axis, slot(buf))
+        take(stage, axis, buf)
         me, n, _ = axes[axis]
         acc = own.astype(jnp.float32)
         for r in range(1, n):
@@ -446,13 +443,13 @@
 
     early = list(pending)
     del pending[:]
-    take(TAP_Z1, "z", slot(kz))
+    take(TAP_Z1, "z", kz)
     ky[my] = summed(kz, nz)
-    push(TAP_Y, "y", lambda i: ky.at[my], slot(ky))
+    push(TAP_Y, "y", lambda i: ky.at[my], ky)
     oy1s[...] = reduced(OUT_Y1, "y", oy1, osend[my]).reshape(nz, rows, LANES)
-    push(OUT_Z2, "z", slot(oy1s), slot(oz2))
+    push(OUT_Z2, "z", slot(oy1s), oz2)
     oz1s[...] = reduced(OUT_Z1, "z", oz1, otail[mz]).reshape(ny // 2, rows, LANES)
-    push(OUT_Y2, "y", lambda i: oz1s.at[lax.rem(i, ny // 2)], slot(oy2))
+    push(OUT_Y2, "y", lambda i: oz1s.at[lax.rem(i, ny // 2)], oy2)
 
     @pl.when(core == 1)
     def _():
@@ -462,7 +459,7 @@
     low = lax.broadcasted_iota(jnp.int32, (FRAMES // 2, LANES), 1) < HALF
 
     def products(i, stage, axis, buf, out):
-        take(stage, axis, slot(buf))
+        take(stage, axis, buf)
         me, n, _ = axes[axis]
         buf[me] = gp[i]
         for k in range(n):
@@ -480,11 +477,11 @@
     for wait in early:
         wait()
     products(1, PROJ_Z, "z", pz, gz1)
-    push(GLU_Y2, "y", slot(gz1), slot(gy2))
+    push(GLU_Y2, "y", slot(gz1), gy2)
     products(0, PROJ_Y, "y", py, gy1)
-    push(GLU_Z2, "z", slot(gy1), slot(gz2))
-
-    take(TAP_Y, "y", slot(ky))
+    push(GLU_Z2, "z", slot(gy1), gz2)
+
+    take(TAP_Y, "y", ky)
     tap_total = summed(ky, ny)
     upper = lax.broadcasted_iota(jnp.int32, (span, LANES), 0) < each
 
@@ -496,7 +493,7 @@
         - per_tile(sums[0:1] / total, sums[1:2] / total) * tap_total[span : 2 * span]
         - per_tile(sums[2:3] / total, sums[3:4] / total) * tap_total[2 * span :]
     )
-    push(TAP_Z2, "z", lambda i: kg.at[mz], slot(kg))
+    push(TAP_Z2, "z", lambda i: kg.at[mz], kg)
 
     @pl.when(core == 0)
     def _():
@@ -510,7 +507,7 @@
     gg_ref[1] = reduced(GLU_Y2, "y", gy2, gz1[my])
     gg_ref[0] = reduced(GLU_Z2, "z", gz2, gy1[mz])
     done(1, gg_ref, gg_hbm)
-    take(TAP_Z2, "z", slot(kg))
+    take(TAP_Z2, "z", kg)
     done(3, kg, kg_hbm)
 
     for wait in pending:
@@ -521,9 +518,7 @@
 
     @pl.when(core == 1)
     def _():
-        @pl.loop(0, nx)
-        def _(i):
-            gather_copy(i).wait_send()
+        every(GATHER, up, (dp, 0, mx)).wait_send()
 
 
 def unpack(gg, og, kg, gb, ig, ig_out, glu_out, out_out, taps_out, gain_out, bias_out):
@@ -570,7 +565,7 @@
     big = pltpu.VMEM((2, FRAMES, LANES), f32)
     padded = pltpu.VMEM((2, FRAMES + 2 * PAD, LANES), f32)
 
-    sem = pltpu.SemaphoreType.DMA((STAGES, max(nx, ny, nz)))
+    sem = pltpu.SemaphoreType.DMA((STAGES,))
     ig, gg, og, kg, gb = pl.pallas_call(
         functools.partial(body, nx, ny, nz),
         out_shape=(

time: 86.3 us -> 83.3 us (0.965)
  the two profiles are of different devices: /device:TPU:8 before, /device:TPU:4 now
where the time goes in v6:
time: 83.3 us; the launch traced here: 83.1 us
  Pallas kernels  81.8 us (98%)
  between operations  1.29 us (2%)
    pallas_call x1, Pallas kernels, shards(): pl.pallas_call(functools.partial(body, nx, ny, nz), out_shape=(jax.ShapeD...  80.3 us

profile of v6, /device:TPU:4, one launch (start us, length us, event | category | flops | bytes accessed | tf_op | source)
XLA Modules:
  0.0 83.1 jit_solution(13932854943433843929)
XLA Ops:
  1.3 80.3 %conformer_backward.1 = (bf16[192,128]{1,0:T(8,128)(2,1)}, f32[2,48,128]{2,1,0:T(8,128)}, f32[2,24,128]{2,1,0:T(8,128)}, f32[8,8,128]{2,1,0:T(8,128)}, f32[8,128]{1,0:T(8,128)}) custom-call(s32[1]{0:T(128)S(6)} %copy.14.cnt_hbm, bf16[128,1536]{1,0:T(8,128)(2,1)} %bitcast.17, bf16[2,192,1536]{2,1,0:T(8,128)(2,1)} %bitcast.15, f32[32,192]{1,0:T(8,128)} %bitcast.19, ...), custom_call_target="tpu_custom_call" | custom-call | tf_op jit(solution)/shard_map/conformer_backward/pallas_call | solution.py:569
  81.6 1.5 %unpack.1 = (bf16[192,128]{1,0:T(8,128)(2,1)}, f32[24,2,192]{2,1,0:T(2,128)}, f32[24,192]{1,0:T(8,128)}, f32[32,192]{1,0:T(8,128)}, f32[1,192]{1,0:T(1,128)}, /*index=5*/f32[1,192]{1,0:T(1,128)}) custom-call(f32[2,48,128]{2,1,0:T(8,128)} %get-tuple-element.17.gg, f32[2,24,128]{2,1,0:T(8,128)} %get-tuple-element.18.og, f32[8,8,128]{2,1,0:T(8,128)} %get-tuple-element.19.kg, ...), custom_call_target="tpu_custom_call" | custom-call | tf_op jit(solution)/shard_map/unpack/pallas_call | solution.py:626

commit v7 on v6

--- a/solution.py
+++ b/solution.py
@@ -97,8 +97,8 @@
     loads = [
         pltpu.make_async_copy(a, b, local_sem.at[i])
         for i, (a, b) in enumerate((
-            (x_hbm, xs), (glu_hbm, glus), (taps_hbm, taps), (gain_hbm, gains),
-            (shift_hbm, shifts), (cnt_hbm, cnt), (out_hbm, outs), (cot_hbm, cots),
+            (taps_hbm, taps), (gain_hbm, gains), (shift_hbm, shifts), (cnt_hbm, cnt),
+            (x_hbm, xs), (glu_hbm, glus), (out_hbm, outs), (cot_hbm, cots),
         ))
     ]
     for load in loads:
@@ -130,7 +130,7 @@
         hs[j, 1, :, HALF:] = zero_half
     gas[1, :, HALF:] = zero_half
     par[1] = jnp.zeros(par.shape[1:], jnp.float32)
-    for load in loads[2:6]:
+    for load in loads[0:4]:
         load.wait()
     count = cnt[0]
     frame = lax.broadcasted_iota(jnp.int32, (FRAMES, LANES), 0)
@@ -139,7 +139,7 @@
         par[0, pl.ds(at, size), :] = ref[:, 0:LANES]
         par[1, pl.ds(at, size), 0:HALF] = ref[:, LANES:]
 
-    for load in loads[0:2]:
+    for load in loads[4:6]:
         load.wait()
     for i in range(2):
         h = lax.dot_general(xs[...], glus[i], WIDE, preferred_element_type=jnp.float32)
@@ -176,17 +176,6 @@
             at = pl.multiple_of(c * LANES, LANES)
             dst[pl.ds(at, LANES), :] = jnp.transpose(src[:, pl.ds(at, LANES)])
 
-    flip(xs, xt)
-
-    @pl.loop(0, nz)
-    def _(z):
-        part = xt[pl.ds(pl.multiple_of(z * slab, slab), slab), :].astype(jnp.float32)
-        xw[z, :, 0:rows, :] = part.reshape(ny, rows, LANES).astype(jnp.bfloat16)
-
-    if xw.shape[2] > rows:
-        xw[:, :, rows:, :] = jnp.zeros((nz, ny, xw.shape[2] - rows, LANES), jnp.bfloat16)
-    xp[0, my] = xw[mx, my]
-    xp[1, mz] = xw[mz, mx]
     in_y = push(IN_Y, "y", lambda i: xw.at[mx, i], xp.at[0], False)
     in_z = push(IN_Z, "z", lambda i: xw.at[i, mx], xp.at[1], False)
     in_x = push(IN_X, "x", lambda i: xc, xg, False)
@@ -213,6 +202,18 @@
 
     pl.semaphore_wait(barrier, (nx - 1) + (ny - 1) + (nz - 1) + nx)
     push(STAT_Y, "y", lambda i: st_y.at[my], st_y)
+
+    flip(xs, xt)
+
+    @pl.loop(0, nz)
+    def _(z):
+        part = xt[pl.ds(pl.multiple_of(z * slab, slab), slab), :].astype(jnp.float32)
+        xw[z, :, 0:rows, :] = part.reshape(ny, rows, LANES).astype(jnp.bfloat16)
+
+    if xw.shape[2] > rows:
+        xw[:, :, rows:, :] = jnp.zeros((nz, ny, xw.shape[2] - rows, LANES), jnp.bfloat16)
+    xp[0, my] = xw[mx, my]
+    xp[1, mz] = xw[mz, mx]
 
     @pl.when(core == 0)
     def _():
@@ -427,9 +428,8 @@
     def _():
         input_grad()
 
-        @pl.loop(0, nx)
-        def _(i):
-            gather_copy(i).start()
+        around("x", lambda i: gather_copy(i).start())
+        gather_copy(mx).start()
 
         share_inputs()
 

time: 83.3 us -> 83.6 us (level)
  no operation moved by 1% of the time
where the time goes in v7:
time: 83.6 us; the launch traced here: 83.4 us
  Pallas kernels  82.1 us (98%)
  between operations  1.29 us (2%)
    pallas_call x1, Pallas kernels, shards(): pl.pallas_call(functools.partial(body, nx, ny, nz), out_shape=(jax.ShapeD...  80.5 us

profile of v7, /device:TPU:4, one launch (start us, length us, event | category | flops | bytes accessed | tf_op | source)
XLA Modules:
  0.0 83.4 jit_solution(15984220176573000780)
XLA Ops:
  1.3 80.5 %conformer_backward.1 = (bf16[192,128]{1,0:T(8,128)(2,1)}, f32[2,48,128]{2,1,0:T(8,128)}, f32[2,24,128]{2,1,0:T(8,128)}, f32[8,8,128]{2,1,0:T(8,128)}, f32[8,128]{1,0:T(8,128)}) custom-call(s32[1]{0:T(128)S(6)} %copy.14.cnt_hbm, bf16[128,1536]{1,0:T(8,128)(2,1)} %bitcast.17, bf16[2,192,1536]{2,1,0:T(8,128)(2,1)} %bitcast.15, f32[32,192]{1,0:T(8,128)} %bitcast.19, ...), custom_call_target="tpu_custom_call" | custom-call | tf_op jit(solution)/shard_map/conformer_backward/pallas_call | solution.py:569
  81.8 1.5 %unpack.1 = (bf16[192,128]{1,0:T(8,128)(2,1)}, f32[24,2,192]{2,1,0:T(2,128)}, f32[24,192]{1,0:T(8,128)}, f32[32,192]{1,0:T(8,128)}, f32[1,192]{1,0:T(1,128)}, /*index=5*/f32[1,192]{1,0:T(1,128)}) custom-call(f32[2,48,128]{2,1,0:T(8,128)} %get-tuple-element.17.gg, f32[2,24,128]{2,1,0:T(8,128)} %get-tuple-element.18.og, f32[8,8,128]{2,1,0:T(8,128)} %get-tuple-element.19.kg, ...), custom_call_target="tpu_custom_call" | custom-call | tf_op jit(solution)/shard_map/unpack/pallas_call | solution.py:626
